TPU v7x, 32 devices: a whole 2x2x4 slice. The times are simulated.
32 devices in a mesh: section: 4 (over y, core), expert: 8 (over z, x).
Axes of the slice: x: 2, y: 2, z: 4, core: 2. Of those that a mesh axis runs over, the one named last changes fastest.
Arguments:
- acts: bfloat16 [4, 512, 2048], P('section', 'expert'), may hold values from -6 to 6
- norm_gains: float32 [4, 2, 2048], P('section'), may hold values from 0.5 to 5.5
- w_query: bfloat16 [4, 2048, 1024], P('section', None, 'expert'), may hold values from -0.125 to 0.125
- w_keyval: bfloat16 [4, 2048, 4, 256], P('section', 'expert'), may hold values from -0.125 to 0.125
- w_out: bfloat16 [4, 1024, 2048], P('section', 'expert'), may hold values from -0.5 to 0.5
- w_gate_up: bfloat16 [4, 32, 2048, 1536], P('section', 'expert'), may hold values from -0.125 to 0.125
- w_down: bfloat16 [4, 32, 768, 2048], P('section', 'expert'), may hold values from -0.21875 to 0.21875
- expert_ids: int32 [4, 512, 8], P('section', 'expert'), may hold values from 0 to 31, all different within a row; in each aligned block of 64 rows (0 to 63, 64 to 127, ..., all dimensions but the last counted through in order) at most 24 rows name the same one
- gate_weights: float32 [4, 512, 8], P('section', 'expert'), may hold values from 0.05 to 0.3
- segment_ids: int32 [4, 512], P('section'), may hold values from 0 to 15, never falling along the last dimension, each value on 1 to 128 neighbouring positions
Outputs:
- handed: bfloat16 [4, 512, 2048], P('section', 'expert')
Inputs may be any that keep to these rules, and one draw needn't show every extreme that they name: `expert_ids`: A token names 8 different experts. In each section the tokens of one index of expert (aligned blocks of 64 tokens) name no expert more than 24 times, a bound that some block reaches. `segment_ids`: never falling along a section's positions; a segment holds at most 128 positions, and one exactly that many.
All inputs are finite; a program needn't handle non-finite values.
Results may differ from a plain program's by a relative error of at most 0.015.
The roundings to bfloat16 on the way count: a program that leaves them out, or rounds other values in their place, can miss the bound.
Values may be sent and summed in bfloat16 or wider, within the bound.
A program may use at most 128 MiB of HBM per device.

v0:
```python
import math

import jax
import jax.numpy as jnp
from jax import lax
from jax.sharding import PartitionSpec as P

HD = 128
KV = 4
EXPERTS = 32
TOPK = 8
CAP = 24


EPS = 1e-06
ROPE_BASE = 1000000.0


def shifted_2(x, axis, by):
    length = lax.axis_size(axis)
    return lax.ppermute(x, axis, [(i, (i + by) % length) for i in range(length)])


def rms_scale(values, gain_row):
    mean_sq = jnp.mean(values * values, axis=-1, keepdims=True)
    return values * lax.rsqrt(mean_sq + EPS) * gain_row


def rotate(values, positions):
    half_width = values.shape[-1] // 2
    frequency = ROPE_BASE ** (-jnp.arange(half_width, dtype=jnp.float32) * 2.0 / values.shape[-1])
    angles = positions[:, None] * frequency[None, :]
    cosines = jnp.cos(angles)[:, None, :]
    sine_table = jnp.sin(angles)[:, None, :]
    leading = values[..., :half_width]
    trailing = values[..., half_width:]
    return jnp.concatenate(
        [leading * cosines - trailing * sine_table, trailing * cosines + leading * sine_table],
        axis=-1,
    )


def head_block(q_block, key_rows, value_rows, seg_block, seg_all, pos_block, pos_all, score_scale):
    scores = (
        jnp.einsum("qhd,kd->hqk", q_block, key_rows, preferred_element_type=jnp.float32)
        * score_scale
    )
    allowed = (seg_block[:, None] == seg_all[None, :]) & (pos_all[None, :] <= pos_block[:, None])
    scores = jnp.where(allowed[None], scores, -1e30)
    row_max = jnp.max(scores, axis=-1, keepdims=True)
    shifted = jnp.exp(scores - row_max)
    probability = (shifted / jnp.sum(shifted, axis=-1, keepdims=True)).astype(jnp.bfloat16)
    return jnp.einsum(
        "hqk,kd->qhd", probability, value_rows, preferred_element_type=jnp.float32
    ).astype(jnp.bfloat16)


def expert_rows(grouped, gate_up, down_proj):
    gate_up_out = jnp.einsum("necd,edf->necf", grouped, gate_up, preferred_element_type=jnp.float32)
    half_width = down_proj.shape[1]
    hidden = (jax.nn.silu(gate_up_out[..., :half_width]) * gate_up_out[..., half_width:]).astype(
        jnp.bfloat16
    )
    return jnp.einsum(
        "necf,efd->necd", hidden, down_proj, preferred_element_type=jnp.float32
    ).astype(jnp.bfloat16)


def send_back(results):
    return lax.all_to_all(results, "expert", split_axis=0, concat_axis=0, tiled=True)


def per_device(
    acts,
    norm_gains,
    w_query,
    w_keyval,
    w_out,
    w_gate_up,
    w_down,
    expert_ids,
    gate_weights,
    segment_ids,
):
    device_count = lax.axis_size("expert")
    my_index = lax.axis_index("expert")
    tok_rows = acts.shape[1]
    width = acts.shape[2]
    head_dev = w_query.shape[2] // HD
    local_experts = w_gate_up.shape[1]
    heads_total = head_dev * device_count
    gains = norm_gains[0]
    x_wide = acts[0].astype(jnp.float32)
    normed = rms_scale(x_wide, gains[0]).astype(jnp.bfloat16)
    kv_index = my_index * head_dev // (heads_total // KV)
    query_weight = w_query[0]
    gathered_keyval = lax.all_gather(w_keyval[0], "expert", axis=0, tiled=True)
    head_keyval = lax.dynamic_index_in_dim(gathered_keyval, kv_index, 1, keepdims=False)
    row_piece = lax.all_gather(normed, "expert", axis=0, tiled=True)
    piece_rows = row_piece.shape[0]
    positions = jnp.arange(piece_rows).astype(jnp.float32)
    query_piece_rows = row_piece.shape[0]
    query_positions = jnp.arange(query_piece_rows).astype(jnp.float32)
    queries = jnp.dot(row_piece, query_weight, preferred_element_type=jnp.float32).reshape(
        query_piece_rows, head_dev, HD
    )
    queries = (
        rotate(queries, query_positions)
        .astype(jnp.bfloat16)
        .reshape(query_piece_rows, head_dev * HD)
    )
    keyval = jnp.dot(row_piece, head_keyval, preferred_element_type=jnp.float32)
    key_rows = rotate(keyval[:, None, :HD], positions).astype(jnp.bfloat16).reshape(piece_rows, HD)
    value_rows = keyval[:, HD:].astype(jnp.bfloat16)
    projected = jnp.concatenate([queries, key_rows, value_rows], axis=1)
    tokens = projected.shape[0]
    all_queries = projected[:, : head_dev * HD].reshape(tokens, head_dev, HD)
    all_keys = projected[:, head_dev * HD : (head_dev + 1) * HD]
    all_values = projected[:, (head_dev + 1) * HD :]
    segments = segment_ids[0]
    all_positions = jnp.arange(tokens)
    q_rows = min(512, tokens)
    score_scale = 1.0 / math.sqrt(HD)

    def attend(first_row):
        q_block = lax.dynamic_slice_in_dim(all_queries, first_row, q_rows, 0)
        seg_block = lax.dynamic_slice_in_dim(segments, first_row, q_rows, 0)
        pos_block = first_row + jnp.arange(q_rows)
        return head_block(
            q_block,
            all_keys,
            all_values,
            seg_block,
            segments,
            pos_block,
            all_positions,
            score_scale,
        )

    block_starts = jnp.arange(tokens // q_rows) * q_rows
    attended = lax.map(attend, block_starts).reshape(tokens, head_dev * HD)
    out_weight = w_out[0]
    attention = lax.psum_scatter(
        jnp.dot(attended, out_weight, preferred_element_type=jnp.float32).astype(jnp.bfloat16),
        "expert",
        scatter_dimension=0,
        tiled=True,
    ).astype(jnp.float32)
    middle_wide = (x_wide + attention).astype(jnp.bfloat16).astype(jnp.float32)
    mixer_in = rms_scale(middle_wide, gains[1]).astype(jnp.bfloat16)
    routes_flat = expert_ids[0].reshape(-1)
    onehot = (routes_flat[:, None] == jnp.arange(EXPERTS, dtype=jnp.int32)[None, :]).astype(
        jnp.int32
    )
    earlier = jnp.cumsum(onehot, axis=0) - onehot
    slot_rank = jnp.sum(earlier * onehot, axis=1)
    slot_index = routes_flat * CAP + slot_rank
    routed = jnp.repeat(mixer_in, TOPK, axis=0)
    send_rows = (
        jnp.zeros((EXPERTS * CAP, width), jnp.bfloat16)
        .at[slot_index]
        .set(routed)
        .reshape(EXPERTS, CAP, width)
    )
    gate_up = w_gate_up[0]
    down_proj = w_down[0]
    received = lax.all_to_all(send_rows, "expert", split_axis=0, concat_axis=0, tiled=True)
    source_count = received.shape[0] // local_experts
    grouped = received.reshape(source_count, local_experts, received.shape[1], width)
    outputs = expert_rows(grouped, gate_up, down_proj)
    returned = send_back(outputs.reshape(received.shape))
    picked = (
        returned.reshape(EXPERTS * CAP, width)[slot_index]
        .astype(jnp.float32)
        .reshape(tok_rows, TOPK, width)
    )
    mixed = jnp.sum(picked * gate_weights[0][:, :, None], axis=1)
    result = (middle_wide + mixed).astype(jnp.bfloat16)
    handed = shifted_2(result, "section", 1)
    return handed[None]


def solution(mesh):
    placed = (
        P("section", "expert", None),
        P("section", None, None),
        P("section", None, "expert"),
        P("section", "expert", None, None),
        P("section", "expert", None),
        P("section", "expert", None, None),
        P("section", "expert", None, None),
        P("section", "expert", None),
        P("section", "expert", None),
        P("section", None),
    )
    return jax.shard_map(
        per_device,
        mesh=mesh,
        in_specs=placed,
        out_specs=P("section", "expert", None),
        check_vma=False,
    )
```

profile of v0, /device:TPU:9, one launch (start us, length us, event | category | flops | bytes accessed | tf_op | source)
XLA Modules:
  0.0 402.1 jit_solution(9805289773962117961)
XLA Ops:
  6.5 0.0 copy-start
  6.5 0.0 all-gather.4.cloned.1.call-start
  6.5 0.8 fusion.77
  7.4 1.1 fusion.34
  8.5 1.8 fusion.36
  10.3 0.0 all-gather.4.cloned.1.call-update
  10.3 0.0 all-gather.6.cloned.1.call-start
  10.3 1.9 copy.12
  12.3 0.0 all-gather.6.cloned.1.call-update
  12.3 0.0 reduce-scatter.2.cloned.1.call-start
  12.4 47.7 %all-gather.4.cloned.1.call-done = bf16[512,2048]{1,0:T(8,128)(2,1)} async-done(((bf16[64,2048]{1,0:T(8,128)(2,1)}), bf16[512,2048]{1,0:T(8,128)(2,1)}) %all-gather.4.cloned.1.call-update) | async-done | bytes 2097168 | tf_op jit(solution)/shard_map/all_gather | solution.py:99
  60.0 2.5 convolution_bitcast_fusion
  62.5 0.0 copy-start.6
  62.5 70.7 %all-gather.6.cloned.1.call-done = bf16[1,2048,4,256]{3,1,2,0:T(8,128)(2,1)} async-done(((bf16[1,256,4,256]{3,1,2,0:T(8,128)(2,1)}), bf16[1,2048,4,256]{3,1,2,0:T(8,128)(2,1)}) %all-gather.6.cloned.1.call-update) | async-done | bytes 4194320 | tf_op jit(solution)/shard_map/all_gather | solution.py:97
  133.3 2.6 fusion.24
  135.9 0.6 fusion.70
  136.5 0.4 fusion.78
  136.9 0.2 fusion.29
  137.1 0.0 copy-done
  137.1 0.0 copy-start.4
  137.1 0.0 copy-start.2
  137.2 2.4 convolution_convert_fusion
  139.5 0.0 reduce-scatter.2.cloned.1.call-update
  139.5 0.1 copy.14
  139.6 0.1 eq.59
  139.7 0.1 eq.55
  139.8 1.2 reduce-window.6
  141.0 0.2 slice_reduce_fusion
  141.3 0.1 copy.13
  141.4 0.1 mul.210
  141.5 0.1 fusion.68
  141.6 64.2 %reduce-scatter.2.cloned.1.call-done = bf16[64,2048]{1,0:T(8,128)(2,1)} async-done(((bf16[512,2048]{1,0:T(8,128)(2,1)}), bf16[64,2048]{1,0:T(8,128)(2,1)}) %reduce-scatter.2.cloned.1.call-update) | async-done | bytes 262160 | tf_op jit(solution)/shard_map/reduce_scatter | solution.py:143
  205.7 1.1 fusion.30
  206.9 1.8 fusion.32
  208.7 5.0 %scatter_custom_fusion = bf16[768,2048]{1,0:T(8,128)(2,1)S(1)} fusion(s32[512]{0:T(512)S(1)} %bitcast.115, bf16[]{:T(256)} %constant.73.clone.1, bf16[64,2048]{1,0:T(8,128)(2,1)} %fusion.32), kind=kCustom, calls=%fused_computation.15 | custom fusion | bytes 3407874 | tf_op jit(solution)/shard_map/scatter | solution.py:162
  213.7 72.9 %all_to_all.10 = bf16[32,24,2048]{2,1,0:T(8,128)(2,1)S(1)} all-to-all(bf16[32,24,2048]{2,1,0:T(8,128)(2,1)S(1)} %bitcast.110), channel_id=1, replica_groups=mesh['section'=4,'expert'=8] {'expert'}, dimensions={0} | all-to-all | bytes 6291456 | tf_op jit(solution)/shard_map/all_to_all | solution.py:167
  286.6 10.8 %fusion.5 = f32[8,4,24,1536]{3,2,0,1:T(8,128)S(1)} fusion(bf16[1,4,2048,1536]{3,2,1,0:T(8,128)(2,1)} %param.15, bf16[8,4,24,2048]{3,2,1,0:T(8,128)(2,1)S(1)} %bitcast.111), kind=kOutput, calls=%fused_computation.8 | convolution fusion | flops 4831838208 | bytes 33030144 | tf_op jit(solution)/shard_map/necd,edf->necf/dot_general | solution.py:59
  297.4 7.3 %fusion.12 = bf16[8,4,24,2048]{3,2,0,1:T(8,128)(2,1)S(1)} fusion(bf16[1,4,768,2048]{3,2,1,0:T(8,128)(2,1)} %param.16, f32[8,4,24,1536]{3,2,0,1:T(8,128)S(1)} %fusion.5), kind=kOutput, calls=%fused_computation.11 | convolution fusion | flops 2421030912 | bytes 20447232 | tf_op jit(solution)/shard_map/necf,efd->necd/dot_general | solution.py:64
  304.7 1.9 copy.18
  306.7 5.5 %all-to-all-start.1 = ((bf16[32,24,2048]{2,1,0:T(8,128)(2,1)}), bf16[32,24,2048]{2,1,0:T(8,128)(2,1)}, u32[]{:S(2)}, u32[]{:S(2)}) async-start(bf16[32,24,2048]{2,1,0:T(8,128)(2,1)} %bitcast.34), calls=%async_computation.2 | async-start | bytes 6291456 | tf_op jit(solution)/shard_map/all_to_all | solution.py:70
  312.1 0.1 copy.19
  312.2 68.9 %all-to-all-done.1 = bf16[32,24,2048]{2,1,0:T(8,128)(2,1)} async-done(((bf16[32,24,2048]{2,1,0:T(8,128)(2,1)}), bf16[32,24,2048]{2,1,0:T(8,128)(2,1)}, u32[]{:S(2)}, u32[]{:S(2)}) %all-to-all-start.1) | async-done | bytes 3145760 | tf_op jit(solution)/shard_map/all_to_all | solution.py:70
  381.2 6.8 %gather_fusion = bf16[512,2048]{1,0:T(8,128)(2,1)S(1)} fusion(bf16[768,2048]{1,0:T(8,128)(2,1)} %bitcast.35, s32[1024]{0:T(1024)S(1)} %pad_clamp_fusion), kind=kCustom, calls=%fused_computation | custom fusion | bytes 4196352 | tf_op jit(solution)/shard_map/gather | solution.py:173
  387.9 1.8 fusion.4
  389.8 0.1 fusion.33
  389.9 1.6 collective-permute-start
  391.5 3.3 collective-permute-done
  394.8 0.7 copy.27
  (20 shorter events, 0.1 us)
Async XLA Ops:
  6.5 130.6 %copy-start = (bf16[1,128,2048]{2,1,0:T(8,128)(2,1)S(1)}, bf16[1,128,2048]{2,1,0:T(8,128)(2,1)}, u32[]{:S(2)}) copy-start(bf16[1,128,2048]{2,1,0:T(8,128)(2,1)} %param.14) | copy-start | bytes 1572868
  6.5 53.5 %all-gather.4.cloned.1.call-start = ((), (), s32[]{:S(2)}) async-start(), calls=%async_computation.3 | async-start | bytes 2359296 | tf_op jit(solution)/shard_map/all_gather | solution.py:99
  10.3 123.0 %all-gather.6.cloned.1.call-start = ((), (), s32[]{:S(2)}) async-start(), calls=%async_computation.5 | async-start | bytes 4718592 | tf_op jit(solution)/shard_map/all_gather | solution.py:97
  12.3 193.5 %reduce-scatter.2.cloned.1.call-start = ((), (), s32[]{:S(2)}) async-start(), calls=%async_computation.4 | async-start | bytes 2359296 | tf_op jit(solution)/shard_map/reduce_scatter | solution.py:143
  62.5 74.0 %copy-start.6 = (s32[1,512]{1,0:T(1,128)S(1)}, s32[1,512]{1,0:T(1,128)}, u32[]{:S(2)}) copy-start(s32[1,512]{1,0:T(1,128)} %param.19) | copy-start | bytes 6148
  137.1 2.4 copy-start.4
  137.1 68.6 %copy-start.2 = (bf16[1,64,2048]{2,1,0:T(8,128)(2,1)S(1)}, bf16[1,64,2048]{2,1,0:T(8,128)(2,1)}, u32[]{:S(2)}) copy-start(bf16[1,64,2048]{2,1,0:T(8,128)(2,1)} %param.10) | copy-start | bytes 786436
  306.7 5.5 %copy-start.5 = (f32[1,64,8]{1,2,0:T(8,128)S(1)}, f32[1,64,8]{1,2,0:T(8,128)}, u32[]{:S(2)}) copy-start(f32[1,64,8]{1,2,0:T(8,128)} %param.18) | copy-start | bytes 6148
  306.7 74.5 %all-to-all-start.1 = ((bf16[32,24,2048]{2,1,0:T(8,128)(2,1)}), bf16[32,24,2048]{2,1,0:T(8,128)(2,1)}, u32[]{:S(2)}, u32[]{:S(2)}) async-start(bf16[32,24,2048]{2,1,0:T(8,128)(2,1)} %bitcast.34), calls=%async_computation.2 | async-start | bytes 6291456 | tf_op jit(solution)/shard_map/all_to_all | solution.py:70
  381.2 8.6 %copy-start.3 = (bf16[64,2048]{1,0:T(8,128)(2,1)S(1)}, bf16[64,2048]{1,0:T(8,128)(2,1)}, u32[]{:S(2)}) copy-start(bf16[64,2048]{1,0:T(8,128)(2,1)} %reduce-scatter.2.cloned.1.call-done) | copy-start | bytes 786436
  381.2 14.4 %copy-start.1 = (bf16[1,128,2048]{2,1,0:T(8,128)(2,1)S(1)}, bf16[1,128,2048]{2,1,0:T(8,128)(2,1)}, u32[]{:S(2)}) copy-start(bf16[1,128,2048]{2,1,0:T(8,128)(2,1)} %param.14) | copy-start | bytes 1572868
  389.9 4.9 %collective-permute-start = (bf16[64,2048]{1,0:T(8,128)(2,1)S(1)}, bf16[64,2048]{1,0:T(8,128)(2,1)S(1)}, u32[]{:S(2)}, u32[]{:S(2)}) collective-permute-start(bf16[64,2048]{1,0:T(8,128)(2,1)S(1)} %fusion.33), channel_id=1, source_target_pairs={{0,8},{8,16},{16,24},{24,0},{1,9},{9,17},{17,25},{25,1},{2,10},{10... | collective-permute-start | bytes 786440 | tf_op jit(solution)/shard_map/ppermute | solution.py:21
Sparse Core Ops, SparseCore 0:
  10.4 49.5 all-gather.3
  62.2 71.0 all-gather.5
  139.7 66.0 reduce-scatter.1
where the time goes:
time: 407 us; the launch traced here: 402 us
  waiting for transfers between devices  255 us (63%)
  blocking collectives  72.9 us (18%)
  matrix products  26 us (6%)
  local copies, waits for them, and re-layouts  18 us (4%)
  between operations  13.3 us (3%)
  other arithmetic  9.89 us (2%)
  starting transfers between devices  7.19 us (2%)
    all_to_all x1, blocking collectives, per_device(): lax.all_to_all(send_rows, 'expert', split_axis=0, concat_axis=0, tiled=True)  72.9 us
    all_gather x1, waiting for transfers between devices, per_device(): gathered_keyval = lax.all_gather(w_keyval[0], 'expert', axis=0, tiled=True)  70.7 us
    all_to_all x1, waiting for transfers between devices, send_back(): lax.all_to_all(results, 'expert', split_axis=0, concat_axis=0, tiled=True)  68.9 us
    reduce_scatter x1, waiting for transfers between devices, per_device(): lax.psum_scatter(jnp.dot(attended, out_weight, preferred_element_type=jnp...  64.2 us
    all_gather x1, waiting for transfers between devices, per_device(): row_piece = lax.all_gather(normed, 'expert', axis=0, tiled=True)  47.7 us
    dot_general x1, matrix products, expert_rows(): jnp.einsum('necd,edf->necf', grouped, gate_up, preferred_element_type=jnp...  10.8 us
  transfers between devices with their start and end apart: 5, of which 5 were waited for; matrix products, arithmetic and copies ran while one was open for 2% of the time, Pallas kernels for 0%

commit v1 on v0

--- a/solution.py
+++ b/solution.py
@@ -3,7 +3,11 @@
 import jax
 import jax.numpy as jnp
 from jax import lax
+from jax.experimental import pallas as pl
+from jax.experimental.pallas import tpu as pltpu
 from jax.sharding import PartitionSpec as P
+
+MESH = pl.DeviceIdType.MESH
 
 HD = 128
 KV = 4
@@ -70,7 +74,7 @@
     return lax.all_to_all(results, "expert", split_axis=0, concat_axis=0, tiled=True)
 
 
-def per_device(
+def per_device_general(
     acts,
     norm_gains,
     w_query,
@@ -180,6 +184,354 @@
     return handed[None]
 
 
+LINE = 4
+GROUP = 8
+
+
+def greet(section_too):
+    section, me = lax.axis_index("section"), lax.axis_index("expert")
+    barrier = pltpu.get_barrier_semaphore()
+    for step in range(1, GROUP):
+        other = lax.rem(me + step, GROUP)
+        pl.semaphore_signal(barrier, inc=1, device_id=(section, other), device_id_type=MESH)
+    count = GROUP - 1
+    if section_too:
+        sections = lax.axis_size("section")
+        for step in (1, sections - 1):
+            other = lax.rem(section + step, sections)
+            pl.semaphore_signal(barrier, inc=1, device_id=(other, me), device_id_type=MESH)
+        count += 2
+    pl.semaphore_wait(barrier, count)
+
+
+def gather_line(z, rows, send_sems, recv_sems):
+    section, me = lax.axis_index("section"), lax.axis_index("expert")
+    x = lax.rem(me, 2)
+    partner = z * 2 + 1 - x
+
+    def copy(shard, to, way):
+        return pltpu.make_async_remote_copy(
+            src_ref=rows.at[shard],
+            dst_ref=rows.at[shard],
+            send_sem=send_sems.at[shard, way],
+            recv_sem=recv_sems.at[shard],
+            device_id=(section, to),
+            device_id_type=MESH,
+        )
+
+    sent = []
+
+    def send(shard, to, way):
+        out = copy(shard, to, way)
+        out.start()
+        sent.append(out)
+
+    own = z * 2 + x
+    if z < LINE - 1:
+        send(own, own + 2, 0)
+    if z > 0:
+        send(own, own - 2, 1)
+    send(own, partner, 2)
+    for far in range(1, LINE):
+        if z - far >= 0:
+            shard = (z - far) * 2 + x
+            copy(shard, partner, 2).wait_recv()
+            if z < LINE - 1:
+                send(shard, own + 2, 0)
+            send(shard, partner, 2)
+        if z + far < LINE:
+            shard = (z + far) * 2 + x
+            copy(shard, partner, 2).wait_recv()
+            if z > 0:
+                send(shard, own - 2, 1)
+            send(shard, partner, 2)
+
+    def finish():
+        for place in range(LINE):
+            copy(place * 2 + 1 - x, partner, 2).wait_recv()
+        for out in sent:
+            out.wait_send()
+
+    return finish
+
+
+LINE_ORDER = ((3, 2, 1, 0), (3, 0, 2, 1), (0, 3, 1, 2), (0, 1, 2, 3))
+
+
+def scatter_line(z, terms, from_pair, from_below, from_above, outgoing, pair_send, pair_recv,
+                 line_send, below_recv, above_recv, total):
+    section, me = lax.axis_index("section"), lax.axis_index("expert")
+    x = lax.rem(me, 2)
+    own = z * 2 + x
+    partner = z * 2 + 1 - x
+    pair_copies = {}
+    for place in LINE_ORDER[z]:
+        pair_copies[place] = pltpu.make_async_remote_copy(
+            src_ref=terms.at[place * 2 + 1 - x],
+            dst_ref=from_pair.at[place],
+            send_sem=pair_send.at[place],
+            recv_sem=pair_recv.at[place],
+            device_id=(section, partner),
+            device_id_type=MESH,
+        )
+        pair_copies[place].start()
+
+    def line_copy(place, up):
+        return pltpu.make_async_remote_copy(
+            src_ref=outgoing.at[place],
+            dst_ref=(from_below if up else from_above).at[place],
+            send_sem=line_send.at[place],
+            recv_sem=(below_recv if up else above_recv).at[place],
+            device_id=(section, own + 2 if up else own - 2),
+            device_id_type=MESH,
+        )
+
+    sent = []
+    for place in LINE_ORDER[z]:
+        pair_copies[place].wait_recv()
+        parts = [terms.at[place * 2 + x], from_pair.at[place]]
+        if place >= z and z > 0:
+            line_copy(place, True).wait_recv()
+            parts.append(from_below.at[place])
+        if place <= z and z < LINE - 1:
+            line_copy(place, False).wait_recv()
+            parts.append(from_above.at[place])
+        value = parts[0][...].astype(jnp.float32)
+        for part in parts[1:]:
+            value = value + part[...].astype(jnp.float32)
+        if place == z:
+            total[...] = value
+        else:
+            outgoing[place] = value.astype(jnp.bfloat16)
+            out = line_copy(place, place > z)
+            out.start()
+            sent.append(out)
+    for place in range(LINE):
+        pair_copies[place].wait_send()
+    for out in sent:
+        out.wait_send()
+
+
+def scatter_scratch(rows, width):
+    slots = pltpu.VMEM((LINE, rows, width), jnp.bfloat16)
+    sems = pltpu.SemaphoreType.DMA((LINE,))
+    return [slots] * 4 + [sems] * 5 + [pltpu.VMEM((rows, width), jnp.float32)]
+
+
+def opening_kernel(acts, gains, keyval, routes, rows, weights, all_routes,
+                   send_sems, recv_sems, keyval_send, keyval_recv, route_send, route_recv,
+                   local_sem):
+    section, me = lax.axis_index("section"), lax.axis_index("expert")
+    rows[me] = rms_scale(acts[...].astype(jnp.float32), gains[0:1, :]).astype(jnp.bfloat16)
+    greet(False)
+    place = me // 2
+    own_weights = pltpu.make_async_copy(keyval.at[place], weights.at[me], local_sem.at[0])
+    own_routes = pltpu.make_async_copy(routes, all_routes.at[me], local_sem.at[1])
+
+    def side_copies():
+        keyval_copies, route_copies = [], []
+        for step in range(1, GROUP):
+            other = lax.rem(me + step, GROUP)
+            keyval_copies.append(pltpu.make_async_remote_copy(
+                src_ref=keyval.at[other // 2],
+                dst_ref=weights.at[me],
+                send_sem=keyval_send.at[step],
+                recv_sem=keyval_recv.at[step],
+                device_id=(section, other),
+                device_id_type=MESH,
+            ))
+            route_copies.append(pltpu.make_async_remote_copy(
+                src_ref=routes,
+                dst_ref=all_routes.at[me],
+                send_sem=route_send.at[step],
+                recv_sem=route_recv.at[step],
+                device_id=(section, other),
+                device_id_type=MESH,
+            ))
+        return keyval_copies + route_copies
+
+    side = side_copies()
+    own_weights.start()
+    own_routes.start()
+    for out in side:
+        out.start()
+    for z in range(LINE):
+
+        @pl.when(place == z)
+        def _(z=z):
+            gather_line(z, rows, send_sems, recv_sems)()
+
+    for out in side:
+        out.wait_recv()
+    for out in side:
+        out.wait_send()
+    own_weights.wait()
+    own_routes.wait()
+
+
+def turning_kernel(terms, acts, gains, rows, middle,
+                   from_pair, from_below, from_above, outgoing, pair_send, pair_recv,
+                   line_send, below_recv, above_recv, total, send_sems, recv_sems):
+    me = lax.axis_index("expert")
+    greet(False)
+    for z in range(LINE):
+
+        @pl.when(me // 2 == z)
+        def _(z=z):
+            scatter_line(z, terms, from_pair, from_below, from_above, outgoing, pair_send,
+                         pair_recv, line_send, below_recv, above_recv, total)
+            joined = (acts[...].astype(jnp.float32) + total[...]).astype(jnp.bfloat16)
+            middle[...] = joined
+            rows[me] = rms_scale(joined.astype(jnp.float32), gains[1:2, :]).astype(jnp.bfloat16)
+            gather_line(z, rows, send_sems, recv_sems)()
+
+
+def closing_kernel(terms, middle, handed,
+                   from_pair, from_below, from_above, outgoing, pair_send, pair_recv,
+                   line_send, below_recv, above_recv, total, result, hand_send, hand_recv):
+    section, me = lax.axis_index("section"), lax.axis_index("expert")
+    greet(True)
+    for z in range(LINE):
+
+        @pl.when(me // 2 == z)
+        def _(z=z):
+            scatter_line(z, terms, from_pair, from_below, from_above, outgoing, pair_send,
+                         pair_recv, line_send, below_recv, above_recv, total)
+
+    result[...] = (middle[...].astype(jnp.float32) + total[...]).astype(jnp.bfloat16)
+    hand = pltpu.make_async_remote_copy(
+        src_ref=result,
+        dst_ref=handed,
+        send_sem=hand_send,
+        recv_sem=hand_recv,
+        device_id=(lax.rem(section + 1, lax.axis_size("section")), me),
+        device_id_type=MESH,
+    )
+    hand.start()
+    hand.wait()
+
+
+def in_vmem(count):
+    return [pl.BlockSpec(memory_space=pltpu.VMEM)] * count
+
+
+def remote_params(collective_id):
+    return pltpu.CompilerParams(
+        collective_id=collective_id, has_side_effects=True, vmem_limit_bytes=40 << 20
+    )
+
+
+def per_device(
+    acts,
+    norm_gains,
+    w_query,
+    w_keyval,
+    w_out,
+    w_gate_up,
+    w_down,
+    expert_ids,
+    gate_weights,
+    segment_ids,
+):
+    my_index = lax.axis_index("expert")
+    tok_rows, width = acts.shape[1:]
+    head_dev = w_query.shape[2] // HD
+    local_experts = w_gate_up.shape[1]
+    gains = norm_gains[0]
+    tokens = tok_rows * GROUP
+    keyval = w_keyval[0].transpose(1, 0, 2)
+    keyval_rows = keyval.shape[1]
+    pairs = tok_rows * TOPK
+    routes = jnp.concatenate(
+        [expert_ids[0].astype(jnp.float32).reshape(-1, 128), gate_weights[0].reshape(-1, 128)]
+    )
+    dma = pltpu.SemaphoreType.DMA
+    row_piece, head_keyval, all_routes = pl.pallas_call(
+        opening_kernel,
+        out_shape=[
+            jax.ShapeDtypeStruct((GROUP, tok_rows, width), jnp.bfloat16),
+            jax.ShapeDtypeStruct((GROUP, keyval_rows, 2 * HD), jnp.bfloat16),
+            jax.ShapeDtypeStruct((GROUP,) + routes.shape, jnp.float32),
+        ],
+        in_specs=in_vmem(4),
+        out_specs=in_vmem(3),
+        scratch_shapes=[
+            dma((GROUP, 3)), dma((GROUP,)), dma((GROUP,)), dma((GROUP,)), dma((GROUP,)),
+            dma((GROUP,)), dma((2,)),
+        ],
+        compiler_params=remote_params(0),
+    )(acts[0], gains, keyval, routes)
+    row_piece = row_piece.reshape(tokens, width)
+    head_keyval = head_keyval.reshape(width, 2 * HD)
+
+    positions = jnp.arange(tokens).astype(jnp.float32)
+    queries = jnp.dot(row_piece, w_query[0], preferred_element_type=jnp.float32)
+    queries = rotate(queries.reshape(tokens, head_dev, HD), positions).astype(jnp.bfloat16)
+    keyval_out = jnp.dot(row_piece, head_keyval, preferred_element_type=jnp.float32)
+    key_rows = rotate(keyval_out[:, None, :HD], positions).astype(jnp.bfloat16).reshape(tokens, HD)
+    value_rows = keyval_out[:, HD:].astype(jnp.bfloat16)
+    segments = segment_ids[0]
+    token_order = jnp.arange(tokens)
+    attended = head_block(
+        queries, key_rows, value_rows, segments, segments, token_order, token_order,
+        1.0 / math.sqrt(HD),
+    ).reshape(tokens, head_dev * HD)
+    terms = jnp.dot(attended, w_out[0], preferred_element_type=jnp.float32).astype(jnp.bfloat16)
+    mixer_rows, middle = pl.pallas_call(
+        turning_kernel,
+        out_shape=[
+            jax.ShapeDtypeStruct((GROUP, tok_rows, width), jnp.bfloat16),
+            jax.ShapeDtypeStruct((tok_rows, width), jnp.bfloat16),
+        ],
+        in_specs=in_vmem(3),
+        out_specs=in_vmem(2),
+        scratch_shapes=scatter_scratch(tok_rows, width) + [dma((GROUP, 3)), dma((GROUP,))],
+        compiler_params=remote_params(1),
+    )(terms.reshape(GROUP, tok_rows, width), acts[0], gains)
+    mixer_rows = mixer_rows.reshape(tokens, width)
+
+    lines = pairs // 128
+    all_ids = all_routes[:, :lines].reshape(tokens, TOPK).astype(jnp.int32)
+    all_gates = all_routes[:, lines:].reshape(tokens, TOPK)
+    experts_here = my_index * local_experts + jnp.arange(local_experts, dtype=jnp.int32)
+    named = all_ids[:, :, None] == experts_here[None, None, :]
+    gates = jnp.sum(jnp.where(named, all_gates[:, :, None], 0.0), axis=1)
+    member = jnp.any(named, axis=1)
+    before = (token_order[:, None] > token_order[None, :]).astype(jnp.bfloat16)
+    rank = jnp.dot(before, member.astype(jnp.bfloat16), preferred_element_type=jnp.float32)
+    slots = GROUP * CAP
+    slot_of = jnp.where(member, rank.astype(jnp.int32), -1).T
+    chosen = slot_of[:, None, :] == jnp.arange(slots, dtype=jnp.int32)[None, :, None]
+    slot_gates = jnp.sum(jnp.where(chosen, gates.T[:, None, :], 0.0), axis=2)
+    chosen = chosen.astype(jnp.bfloat16)
+    grouped = jnp.einsum(
+        "est,td->esd", chosen, mixer_rows, preferred_element_type=jnp.float32
+    ).astype(jnp.bfloat16)
+    gate_up_out = jnp.einsum(
+        "esd,edf->esf", grouped, w_gate_up[0], preferred_element_type=jnp.float32
+    )
+    ff = w_down.shape[2]
+    hidden = (jax.nn.silu(gate_up_out[..., :ff]) * gate_up_out[..., ff:]).astype(jnp.bfloat16)
+    outputs = jnp.einsum("esf,efd->esd", hidden, w_down[0], preferred_element_type=jnp.float32)
+    outputs = (outputs * slot_gates[:, :, None]).astype(jnp.bfloat16)
+    mixed = jnp.dot(
+        chosen.reshape(local_experts * slots, tokens).T,
+        outputs.reshape(local_experts * slots, width),
+        preferred_element_type=jnp.float32,
+    ).astype(jnp.bfloat16)
+
+    handed = pl.pallas_call(
+        closing_kernel,
+        out_shape=jax.ShapeDtypeStruct((tok_rows, width), jnp.bfloat16),
+        in_specs=in_vmem(2),
+        out_specs=pl.BlockSpec(memory_space=pltpu.VMEM),
+        scratch_shapes=scatter_scratch(tok_rows, width)
+        + [pltpu.VMEM((tok_rows, width), jnp.bfloat16), dma, dma],
+        compiler_params=remote_params(2),
+    )(mixed.reshape(GROUP, tok_rows, width), middle)
+    return handed[None]
+
+
 def solution(mesh):
     placed = (
         P("section", "expert", None),
@@ -194,7 +546,7 @@
         P("section", None),
     )
     return jax.shard_map(
-        per_device,
+        per_device if mesh.shape["expert"] == GROUP else per_device_general,
         mesh=mesh,
         in_specs=placed,
         out_specs=P("section", "expert", None),

time: 407 us -> 186 us (0.46); the launches traced: 402 us -> 186 us
  waiting for transfers between devices: 255 us -> 0 us
  Pallas kernels: 0 us -> 146 us
  blocking collectives: 72.9 us -> 0 us
  between operations: 13.3 us -> 0.23 us
  local copies, waits for them, and re-layouts: 18 us -> 7.45 us
  other arithmetic: 9.89 us -> 2.03 us
  starting transfers between devices: 7.19 us -> 0 us
  matrix products: 26 us -> 30.5 us
    pallas_call x0 -> x3, Pallas kernels: none -> 146 us  [the longest x1 57.5 us: per_device(): pl.pallas_call(turning_kernel, out_shape=[jax.ShapeDtypeStruct((GROUP, to...]
    all_gather x2 -> x0, waiting for transfers between devices: 118 us -> none  [the longest x1 70.7 us: per_device(): gathered_keyval = lax.all_gather(w_keyval[0], 'expert', axis=0, tiled=True)]
    all_to_all x1 -> x0, blocking collectives: 72.9 us -> none  [per_device(): lax.all_to_all(send_rows, 'expert', split_axis=0, concat_axis=0, tiled=True)]
    all_to_all x1 -> x0, waiting for transfers between devices: 68.9 us -> none  [send_back(): lax.all_to_all(results, 'expert', split_axis=0, concat_axis=0, tiled=True)]
    reduce_scatter x1 -> x0, waiting for transfers between devices: 64.2 us -> none  [per_device(): lax.psum_scatter(jnp.dot(attended, out_weight, preferred_element_type=jnp...]
    gather x1 -> x0, local copies, waits for them, and re-layouts: 6.77 us -> none  [per_device(): returned.reshape(EXPERTS * CAP, width)[slot_index].astype(jnp.float32)]
    all_to_all x1 -> x0, starting transfers between devices: 5.49 us -> none  [send_back(): lax.all_to_all(results, 'expert', split_axis=0, concat_axis=0, tiled=True)]
    scatter x1 -> x0, local copies, waits for them, and re-layouts: 5.01 us -> none  [per_device(): send_rows = jnp.zeros((EXPERTS * CAP, width), jnp.bfloat16).at[slot_index...]
  transfers between devices with their start and end apart: 5 -> 0, of which waited for: 5 -> 0; matrix products, arithmetic and copies ran while one was open for 2% -> 0% of each run, Pallas kernels for 0% -> 0%
where the time goes in v1:
time: 186 us
  Pallas kernels  146 us (78%)
  matrix products  30.5 us (16%)
  local copies, waits for them, and re-layouts  7.45 us (4%)
  other arithmetic  2.03 us (1%)
    pallas_call x1, Pallas kernels, per_device(): pl.pallas_call(turning_kernel, out_shape=[jax.ShapeDtypeStruct((GROUP, to...  57.5 us
    pallas_call x1, Pallas kernels, per_device(): pl.pallas_call(opening_kernel, out_shape=[jax.ShapeDtypeStruct((GROUP, to...  45.3 us
    pallas_call x1, Pallas kernels, per_device(): pl.pallas_call(closing_kernel, out_shape=jax.ShapeDtypeStruct((tok_rows,...  42.9 us
    dot_general x1, matrix products, per_device(): jnp.einsum('esd,edf->esf', grouped, w_gate_up[0], preferred_element_type=...  15.2 us
    dot_general x1, matrix products, per_device(): jnp.dot(chosen.reshape(local_experts * slots, tokens).T, outputs.reshape(...  10.8 us
    unnamed x23, local copies, waits for them, and re-layouts  6.63 us

profile of v1, /device:TPU:9, one launch (start us, length us, event | category | flops | bytes accessed | tf_op | source)
XLA Modules:
  0.0 186.0 jit_solution(7027354344705792660)
XLA Ops:
  0.0 0.0 copy-start
  0.0 0.7 convert_element_type.81
  0.8 0.1 copy.18
  0.9 0.1 convert_element_type.82
  1.0 0.8 copy.19
  1.7 0.1 reshape_squeeze.3
  1.8 1.1 copy.23
  3.0 0.0 copy-start.1
  3.0 0.9 copy-done.1
  3.9 0.0 copy-start.3
  3.9 0.7 copy-done.3
  4.6 0.0 copy-start.7
  4.6 45.3 %shard_map.103 = (bf16[8,64,2048]{2,1,0:T(8,128)(2,1)S(1)}, bf16[8,256,256]{2,1,0:T(8,128)(2,1)S(1)}, f32[8,8,128]{2,1,0:T(8,128)S(1)}) custom-call(bf16[64,2048]{1,0:T(8,128)(2,1)S(1)} %bitcast.77, f32[2,2048]{1,0:T(2,128)S(1)} %bitcast.80, bf16[4,256,256]{2,1,0:T(8,128)(2,1)S(1)} %bitcast.76, f32[8,128]{1,0:T(8,128)S(1)} %pad_maximum_fusion.routes), custom_call_target="tpu_custom_call" | custom-call | tf_op jit(solution)/shard_map/pallas_call | solution.py:449
  49.9 0.8 fusion.60
  50.7 0.0 copy-done.7
  50.7 0.0 copy-start.8
  50.7 0.0 copy-start.9
  50.7 0.8 convolution_bitcast_fusion
  51.5 0.2 convert_element_type.84
  51.7 0.1 copy.20
  51.8 0.1 compare_reduce_fusion
  51.9 0.2 fusion.17
  52.1 0.2 broadcast_in_dim.41
  52.3 0.1 copy.21
  52.4 0.1 fusion.51
  52.5 0.2 select_reduce_fusion
  52.8 0.0 copy-done.8
  52.8 0.6 fusion.53
  53.4 0.0 copy-done.9
  53.4 0.4 fusion.59
  53.8 0.0 copy-start.6
  53.8 1.0 copy-done.6
  54.8 0.2 fusion.19
  55.0 0.0 copy-done
  55.0 0.0 copy-start.2
  55.0 0.0 copy-start.4
  55.0 2.3 %convolution_convert_fusion.1 = bf16[512,2048]{1,0:T(8,128)(2,1)S(1)} fusion(bf16[1,128,2048]{2,1,0:T(8,128)(2,1)S(1)} %copy-done, f32[1,512,512]{1,2,0:T(8,128)} %copy-done.6, f32[512]{0:T(512)S(1)} %fusion.19, f32[512]{0:T(512)S(1)} %get-tuple-element.23, f32[512,256]{0,1:T(8,128)} %copy-done.8), kind=kOutput, calls=%fused_computation.8 | convolution fusion | flops 337444864 | bytes 3805184 | tf_op jit(solution)/shard_map/dot_general | solution.py:479
  57.4 0.0 copy-done.2
  57.4 0.0 copy-done.4
  57.4 57.5 %shard_map.104 = (bf16[8,64,2048]{2,1,0:T(8,128)(2,1)S(1)}, bf16[64,2048]{1,0:T(8,128)(2,1)S(1)}) custom-call(bf16[8,64,2048]{2,1,0:T(8,128)(2,1)S(1)} %bitcast.73, bf16[64,2048]{1,0:T(8,128)(2,1)S(1)} %bitcast.78, f32[2,2048]{1,0:T(2,128)S(1)} %bitcast.81), custom_call_target="tpu_custom_call" | custom-call | tf_op jit(solution)/shard_map/pallas_call | solution.py:480
  115.0 0.0 copy-start.5
  115.0 1.4 copy-done.5
  116.3 15.2 %fusion = f32[4,192,1536]{2,1,0:T(8,128)} fusion(bf16[1,4,2048,1536]{3,2,1,0:T(8,128)(2,1)} %param.15, bf16[512,2048,1]{1,0,2:T(8,128)(2,1)} %bitcast.82, s32[4,512]{1,0:T(4,128)S(1)} %fusion.17), kind=kOutput, calls=%fused_computation | convolution fusion | flops 6444417024 | bytes 31989760 | tf_op jit(solution)/shard_map/esd,edf->esf/dot_general | solution.py:510
  131.5 10.8 %bitcast_convert_fusion = bf16[512,2048]{1,0:T(8,128)(2,1)S(1)} fusion(bf16[1,4,768,2048]{3,2,1,0:T(8,128)(2,1)} %param.16, f32[4,192]{1,0:T(4,128)S(1)} %select_reduce_fusion, f32[4,192,1536]{2,1,0:T(8,128)} %fusion, s32[4,512]{1,0:T(4,128)S(1)} %fusion.17), kind=kOutput, calls=%fused_computation.5 | convolution fusion | flops 4034658304 | bytes 19409920 | tf_op jit(solution)/shard_map/dot_general | solution.py:517
  142.4 42.9 %shard_map.105 = bf16[64,2048]{1,0:T(8,128)(2,1)S(1)} custom-call(bf16[8,64,2048]{2,1,0:T(8,128)(2,1)S(1)} %bitcast.72, bf16[64,2048]{1,0:T(8,128)(2,1)S(1)} %get-tuple-element.14.middle), custom_call_target="tpu_custom_call" | custom-call | tf_op jit(solution)/shard_map/pallas_call | solution.py:523
  185.3 0.7 copy.25
  (6 shorter events, 0.1 us)
Async XLA Ops:
  0.0 55.0 %copy-start = (bf16[1,128,2048]{2,1,0:T(8,128)(2,1)S(1)}, bf16[1,128,2048]{2,1,0:T(8,128)(2,1)}, u32[]{:S(2)}) copy-start(bf16[1,128,2048]{2,1,0:T(8,128)(2,1)} %param.14) | copy-start | bytes 1572868
  3.0 1.0 copy-start.1
  3.9 0.7 copy-start.3
  4.6 46.0 %copy-start.7 = (bf16[1,2048,128]{2,1,0:T(8,128)(2,1)S(1)}, bf16[1,2048,128]{2,1,0:T(8,128)(2,1)}, u32[]{:S(2)}) copy-start(bf16[1,2048,128]{2,1,0:T(8,128)(2,1)} %param.12) | copy-start | bytes 1572868
  50.7 2.1 %copy-start.8 = (f32[512,256]{0,1:T(8,128)}, f32[512,256]{0,1:T(8,128)S(1)}, u32[]{:S(2)}) copy-start(f32[512,256]{0,1:T(8,128)S(1)} %fusion.60) | copy-start | bytes 1572868
  50.7 2.8 %copy-start.9 = (s32[1,512]{1,0:T(1,128)S(1)}, s32[1,512]{1,0:T(1,128)}, u32[]{:S(2)}) copy-start(s32[1,512]{1,0:T(1,128)} %param.19) | copy-start | bytes 6148
  53.8 1.0 copy-start.6
  55.0 2.4 %copy-start.2 = (bf16[1,64,2048]{2,1,0:T(8,128)(2,1)S(1)}, bf16[1,64,2048]{2,1,0:T(8,128)(2,1)}, u32[]{:S(2)}) copy-start(bf16[1,64,2048]{2,1,0:T(8,128)(2,1)} %param.10) | copy-start | bytes 786436
  55.0 2.4 %copy-start.4 = (f32[1,2,2048]{2,1,0:T(2,128)S(1)}, f32[1,2,2048]{2,1,0:T(2,128)}, u32[]{:S(2)}) copy-start(f32[1,2,2048]{2,1,0:T(2,128)} %param.11) | copy-start | bytes 49156
  115.0 1.4 copy-start.5

commit v2 on v0

--- a/solution.py
+++ b/solution.py
@@ -1,9 +1,14 @@
+import functools
 import math
 
 import jax
 import jax.numpy as jnp
 from jax import lax
+from jax.experimental import pallas as pl
+from jax.experimental.pallas import tpu as pltpu
 from jax.sharding import PartitionSpec as P
+
+MESH = pl.DeviceIdType.MESH
 
 HD = 128
 KV = 4
@@ -70,7 +75,7 @@
     return lax.all_to_all(results, "expert", split_axis=0, concat_axis=0, tiled=True)
 
 
-def per_device(
+def per_device_general(
     acts,
     norm_gains,
     w_query,
@@ -180,6 +185,491 @@
     return handed[None]
 
 
+LINE = 4
+GROUP = 8
+CHUNKS = 4
+
+
+def remote(src, dst, send_sem, recv_sem, expert, section=None):
+    if section is None:
+        section = lax.axis_index("section")
+    return pltpu.make_async_remote_copy(
+        src_ref=src,
+        dst_ref=dst,
+        send_sem=send_sem,
+        recv_sem=recv_sem,
+        device_id=(section, expert),
+        device_id_type=MESH,
+    )
+
+
+def greet(section_too):
+    section, me = lax.axis_index("section"), lax.axis_index("expert")
+    barrier = pltpu.get_barrier_semaphore()
+    for step in range(1, GROUP):
+        other = lax.rem(me + step, GROUP)
+        pl.semaphore_signal(barrier, inc=1, device_id=(section, other), device_id_type=MESH)
+    count = GROUP - 1
+    if section_too:
+        sections = lax.axis_size("section")
+        for step in (1, sections - 1):
+            other = lax.rem(section + step, sections)
+            pl.semaphore_signal(barrier, inc=1, device_id=(other, me), device_id_type=MESH)
+        count += 2
+    pl.semaphore_wait(barrier, count)
+
+
+def at_place(body):
+    me = lax.axis_index("expert")
+    x = lax.rem(me, 2)
+    for z in range(LINE):
+
+        @pl.when(me // 2 == z)
+        def _(z=z):
+            body(z, x, z * 2 + x, z * 2 + 1 - x)
+
+
+class Gather:
+    def __init__(self, rows, send_sems, recv_sems):
+        self.rows, self.send_sems, self.recv_sems = rows, send_sems, recv_sems
+
+    def copy(self, chunk, shard, to, way):
+        return remote(
+            self.rows.at[chunk, shard], self.rows.at[chunk, shard],
+            self.send_sems.at[chunk, shard, way], self.recv_sems.at[chunk, shard], to,
+        )
+
+    def first(self, chunk, z, own, partner):
+        out = []
+        if z < LINE - 1:
+            out.append(self.copy(chunk, own, own + 2, 0))
+        if z > 0:
+            out.append(self.copy(chunk, own, own - 2, 1))
+        return out + [self.copy(chunk, own, partner, 2)]
+
+    def passing(self, chunk, z, x, own, partner):
+        out = []
+        for far in range(1, LINE):
+            if z - far >= 0:
+                shard = (z - far) * 2 + x
+                onward = [self.copy(chunk, shard, own + 2, 0)] if z < LINE - 1 else []
+                out.append((shard, onward + [self.copy(chunk, shard, partner, 2)]))
+            if z + far < LINE:
+                shard = (z + far) * 2 + x
+                onward = [self.copy(chunk, shard, own - 2, 1)] if z > 0 else []
+                out.append((shard, onward + [self.copy(chunk, shard, partner, 2)]))
+        return out
+
+    def start(self, chunk, z, x, own, partner):
+        for out in self.first(chunk, z, own, partner):
+            out.start()
+
+    def forward(self, chunk, z, x, own, partner):
+        for shard, onward in self.passing(chunk, z, x, own, partner):
+            self.copy(chunk, shard, partner, 2).wait_recv()
+            for out in onward:
+                out.start()
+
+    def arrive(self, chunk, z, x, own, partner):
+        for place in range(LINE):
+            self.copy(chunk, place * 2 + 1 - x, partner, 2).wait_recv()
+
+    def drain(self, chunk, z, x, own, partner):
+        for out in self.first(chunk, z, own, partner):
+            out.wait_send()
+        for _, onward in self.passing(chunk, z, x, own, partner):
+            for out in onward:
+                out.wait_send()
+
+
+LINE_ORDER = ((3, 2, 1, 0), (3, 0, 2, 1), (0, 3, 1, 2), (0, 1, 2, 3))
+
+
+class Scatter:
+    def __init__(self, terms, total, from_pair, from_below, from_above, outgoing, pair_send,
+                 pair_recv, line_send, below_recv, above_recv):
+        self.terms, self.total = terms, total
+        self.from_pair, self.from_below, self.from_above = from_pair, from_below, from_above
+        self.outgoing = outgoing
+        self.pair_send, self.pair_recv = pair_send, pair_recv
+        self.line_send, self.below_recv, self.above_recv = line_send, below_recv, above_recv
+
+    def pair_copy(self, chunk, place, x, partner):
+        return remote(
+            self.terms.at[chunk, place * 2 + 1 - x], self.from_pair.at[chunk, place],
+            self.pair_send.at[chunk, place], self.pair_recv.at[chunk, place], partner,
+        )
+
+    def line_copy(self, chunk, place, up, own):
+        landing, sems = (
+            (self.from_below, self.below_recv) if up else (self.from_above, self.above_recv)
+        )
+        return remote(
+            self.outgoing.at[chunk, place], landing.at[chunk, place],
+            self.line_send.at[chunk, place], sems.at[chunk, place],
+            own + 2 if up else own - 2,
+        )
+
+    def start(self, chunk, z, x, own, partner):
+        for place in LINE_ORDER[z]:
+            self.pair_copy(chunk, place, x, partner).start()
+
+    def reduce(self, chunk, z, x, own, partner):
+        for place in LINE_ORDER[z]:
+            self.pair_copy(chunk, place, x, partner).wait_recv()
+            parts = [self.from_pair.at[chunk, place]]
+            if place >= z and z > 0:
+                self.line_copy(chunk, place, True, own).wait_recv()
+                parts.append(self.from_below.at[chunk, place])
+            if place <= z and z < LINE - 1:
+                self.line_copy(chunk, place, False, own).wait_recv()
+                parts.append(self.from_above.at[chunk, place])
+            value = self.terms[chunk, place * 2 + x].astype(jnp.float32)
+            for part in parts:
+                value = value + part[...].astype(jnp.float32)
+            if place == z:
+                self.total[chunk] = value
+            else:
+                self.outgoing[chunk, place] = value.astype(jnp.bfloat16)
+                self.line_copy(chunk, place, place > z, own).start()
+
+    def drain(self, chunk, z, x, own, partner):
+        for place in range(LINE):
+            self.pair_copy(chunk, place, x, partner).wait_send()
+            if place != z:
+                self.line_copy(chunk, place, place > z, own).wait_send()
+
+
+def scatter_scratch(rows, columns):
+    slots = pltpu.VMEM((CHUNKS, LINE, rows, columns), jnp.bfloat16)
+    sems = pltpu.SemaphoreType.DMA((CHUNKS, LINE))
+    return [slots] * 4 + [sems] * 5
+
+
+def opening_kernel(acts, gains, keyval, gates, rows, weights, all_gates,
+                   send_sems, recv_sems, keyval_send, keyval_recv, pass_send, gate_send,
+                   gate_recv, local_sem):
+    section, me = lax.axis_index("section"), lax.axis_index("expert")
+    rows[0, me] = rms_scale(acts[...].astype(jnp.float32), gains[0:1, :]).astype(jnp.bfloat16)
+    greet(False)
+    gather = Gather(rows, send_sems, recv_sems)
+    own_gates = pltpu.make_async_copy(gates.at[me], all_gates.at[me], local_sem.at[1])
+    own_weights = pltpu.make_async_copy(keyval.at[me // 2], weights.at[me], local_sem.at[0])
+    gate_copies = []
+    for step in range(1, GROUP):
+        other = lax.rem(me + step, GROUP)
+        gate_copies.append(
+            remote(gates.at[other], all_gates.at[me], gate_send.at[step], gate_recv.at[step], other)
+        )
+
+    def line_weights(place, z, own):
+        return remote(
+            keyval.at[place], weights.at[own], keyval_send.at[place], keyval_recv.at[own],
+            own + 2 * (place - z),
+        )
+
+    def pass_weights(place, z, x, partner):
+        shard = place * 2 + x
+        source = keyval.at[z] if place == z else weights.at[shard]
+        return remote(source, weights.at[shard], pass_send.at[place], keyval_recv.at[shard], partner)
+
+    def begin(z, x, own, partner):
+        gather.start(0, z, x, own, partner)
+        for place in LINE_ORDER[z]:
+            if place != z:
+                line_weights(place, z, own).start()
+        pass_weights(z, z, x, partner).start()
+
+    def through(z, x, own, partner):
+        nearest = sorted((p for p in range(LINE) if p != z), key=lambda p: abs(p - z))
+        for place, (shard, onward) in zip(nearest, gather.passing(0, z, x, own, partner)):
+            gather.copy(0, shard, partner, 2).wait_recv()
+            for out in onward:
+                out.start()
+            source = place * 2 + x
+            remote(
+                weights.at[source], weights.at[source], pass_send.at[place],
+                keyval_recv.at[source], partner,
+            ).wait_recv()
+            pass_weights(place, z, x, partner).start()
+        gather.arrive(0, z, x, own, partner)
+        for place in range(LINE):
+            source = place * 2 + 1 - x
+            remote(
+                weights.at[source], weights.at[source], pass_send.at[place],
+                keyval_recv.at[source], partner,
+            ).wait_recv()
+        gather.drain(0, z, x, own, partner)
+        for place in range(LINE):
+            if place != z:
+                line_weights(place, z, own).wait_send()
+            pass_weights(place, z, x, partner).wait_send()
+
+    at_place(begin)
+    own_weights.start()
+    own_gates.start()
+    for out in gate_copies:
+        out.start()
+    at_place(through)
+    for out in gate_copies:
+        out.wait_recv()
+    for out in gate_copies:
+        out.wait_send()
+    own_weights.wait()
+    own_gates.wait()
+
+
+def closing_kernel(terms, acts, gains, chosen, chosen_t, slot_gates, w_gate_up, w_down, handed,
+                   gate_up, down, work, rows, middle, hidden_sums, hidden, scaled, total, result,
+                   *more):
+    first_scratch, more = more[:9], more[9:]
+    last_scratch, more = more[:9], more[9:]
+    send_sems, recv_sems, work_sems, up_sems, down_sems, hand_send, hand_recv = more
+    section, me = lax.axis_index("section"), lax.axis_index("expert")
+    columns = work.shape[-1]
+    tok_rows = work.shape[-2]
+    tokens = GROUP * tok_rows
+    local_experts = gate_up.shape[0]
+    ff = hidden.shape[-1]
+    first = Scatter(work, total, *first_scratch)
+    last = Scatter(work, total, *last_scratch)
+    gather = Gather(rows, send_sems, recv_sems)
+
+    def part(chunk):
+        return pl.ds(chunk * columns, columns)
+
+    loads = [
+        pltpu.make_async_copy(terms.at[:, :, part(c)], work.at[c], work_sems.at[c])
+        for c in range(CHUNKS)
+    ]
+    up_loads = [
+        pltpu.make_async_copy(w_gate_up.at[:, part(c), :], gate_up.at[:, part(c), :], up_sems.at[c])
+        for c in range(CHUNKS)
+    ]
+    down_loads = [
+        pltpu.make_async_copy(w_down.at[:, :, part(c)], down.at[c % 2], down_sems.at[c % 2])
+        for c in range(CHUNKS)
+    ]
+    for load in loads:
+        load.start()
+    for load in up_loads + down_loads[:2]:
+        load.start()
+    greet(True)
+    for c in range(CHUNKS):
+        loads[c].wait()
+        at_place(functools.partial(first.start, c))
+
+    def first_sums(z, x, own, partner):
+        for c in range(CHUNKS):
+            first.reduce(c, z, x, own, partner)
+        for c in range(CHUNKS):
+            first.drain(c, z, x, own, partner)
+
+    at_place(first_sums)
+    squares = jnp.zeros((tok_rows, 1), jnp.float32)
+    for c in range(CHUNKS):
+        joined = (acts[:, part(c)].astype(jnp.float32) + total[c]).astype(jnp.bfloat16)
+        middle[c] = joined
+        wide = joined.astype(jnp.float32)
+        squares = squares + jnp.sum(wide * wide, axis=-1, keepdims=True)
+    scale = lax.rsqrt(squares / (CHUNKS * columns) + EPS)
+    for c in range(CHUNKS):
+        rows[c, me] = (middle[c].astype(jnp.float32) * scale * gains[1:2, part(c)]).astype(
+            jnp.bfloat16
+        )
+        at_place(functools.partial(gather.start, c))
+
+    def gate_up_chunk(c):
+        up_loads[c].wait()
+        all_rows = rows[c].reshape(tokens, columns)
+
+        @pl.loop(0, local_experts)
+        def _(e):
+            grouped = jnp.dot(chosen[e], all_rows, preferred_element_type=jnp.float32)
+            product = jnp.dot(
+                grouped.astype(jnp.bfloat16), gate_up[e, part(c), :],
+                preferred_element_type=jnp.float32,
+            )
+            if c == 0:
+                hidden_sums[e] = product
+            else:
+                hidden_sums[e] += product
+
+    at_place(functools.partial(gather.forward, 0))
+    for c in range(CHUNKS):
+        if c + 1 < CHUNKS:
+            at_place(functools.partial(gather.forward, c + 1))
+        at_place(functools.partial(gather.arrive, c))
+        gate_up_chunk(c)
+
+    @pl.loop(0, local_experts)
+    def _(e):
+        gate = hidden_sums[e, :, :ff]
+        hidden[e] = (gate / (1.0 + jnp.exp(-gate)) * hidden_sums[e, :, ff:]).astype(jnp.bfloat16)
+
+    slots = hidden.shape[1]
+
+    def down_chunk(c):
+        down_loads[c].wait()
+
+        @pl.loop(0, local_experts)
+        def _(e):
+            out = jnp.dot(hidden[e], down[c % 2, e], preferred_element_type=jnp.float32)
+            scaled[pl.ds(pl.multiple_of(e * slots, slots), slots), :] = (
+                out * slot_gates[e]
+            ).astype(jnp.bfloat16)
+
+        if c + 2 < CHUNKS:
+            down_loads[c + 2].start()
+
+        @pl.loop(0, GROUP)
+        def _(block):
+            work[c, block] = jnp.dot(
+                chosen_t[block], scaled[...], preferred_element_type=jnp.float32
+            ).astype(jnp.bfloat16)
+
+        at_place(functools.partial(last.start, c))
+
+    def hand(c):
+        return remote(
+            result.at[:, part(c)], handed.at[:, part(c)], hand_send.at[c], hand_recv.at[c],
+            me, lax.rem(section + 1, lax.axis_size("section")),
+        )
+
+    def last_sums(c):
+        at_place(functools.partial(last.reduce, c))
+        result[:, part(c)] = (middle[c].astype(jnp.float32) + total[c]).astype(jnp.bfloat16)
+        hand(c).start()
+
+    down_chunk(0)
+    for c in range(CHUNKS):
+        if c + 1 < CHUNKS:
+            down_chunk(c + 1)
+        last_sums(c)
+
+    def drain(z, x, own, partner):
+        for c in range(CHUNKS):
+            gather.drain(c, z, x, own, partner)
+            last.drain(c, z, x, own, partner)
+
+    at_place(drain)
+    for c in range(CHUNKS):
+        hand(c).wait()
+
+
+def in_vmem(count):
+    return [pl.BlockSpec(memory_space=pltpu.VMEM)] * count
+
+
+def remote_params(collective_id, mebibytes):
+    return pltpu.CompilerParams(
+        collective_id=collective_id, has_side_effects=True, vmem_limit_bytes=mebibytes << 20
+    )
+
+
+def per_device(
+    acts,
+    norm_gains,
+    w_query,
+    w_keyval,
+    w_out,
+    w_gate_up,
+    w_down,
+    expert_ids,
+    gate_weights,
+    segment_ids,
+):
+    tok_rows, width = acts.shape[1:]
+    head_dev = w_query.shape[2] // HD
+    local_experts = w_gate_up.shape[1]
+    gains = norm_gains[0]
+    tokens = tok_rows * GROUP
+    keyval = w_keyval[0].transpose(1, 0, 2)
+    keyval_rows = keyval.shape[1]
+    named = expert_ids[0][:, :, None] == jnp.arange(EXPERTS, dtype=jnp.int32)[None, None, :]
+    dense_gates = jnp.sum(jnp.where(named, gate_weights[0][:, :, None], 0.0), axis=1)
+    dense_gates = dense_gates.T.reshape(GROUP, local_experts, tok_rows)
+    dma = pltpu.SemaphoreType.DMA
+    row_piece, head_keyval, all_gates = pl.pallas_call(
+        opening_kernel,
+        out_shape=[
+            jax.ShapeDtypeStruct((1, GROUP, tok_rows, width), jnp.bfloat16),
+            jax.ShapeDtypeStruct((GROUP, keyval_rows, 2 * HD), jnp.bfloat16),
+            jax.ShapeDtypeStruct(dense_gates.shape, jnp.float32),
+        ],
+        in_specs=in_vmem(4),
+        out_specs=in_vmem(3),
+        scratch_shapes=[
+            dma((1, GROUP, 3)), dma((1, GROUP)), dma((LINE,)), dma((GROUP,)), dma((LINE,)),
+            dma((GROUP,)), dma((GROUP,)), dma((2,)),
+        ],
+        compiler_params=remote_params(0, 40),
+    )(acts[0], gains, keyval, dense_gates)
+    row_piece = row_piece.reshape(tokens, width)
+    head_keyval = head_keyval.reshape(width, 2 * HD)
+
+    positions = jnp.arange(tokens).astype(jnp.float32)
+    queries = jnp.dot(row_piece, w_query[0], preferred_element_type=jnp.float32)
+    queries = rotate(queries.reshape(tokens, head_dev, HD), positions).astype(jnp.bfloat16)
+    keyval_out = jnp.dot(row_piece, head_keyval, preferred_element_type=jnp.float32)
+    key_rows = rotate(keyval_out[:, None, :HD], positions).astype(jnp.bfloat16).reshape(tokens, HD)
+    value_rows = keyval_out[:, HD:].astype(jnp.bfloat16)
+    segments = segment_ids[0]
+    token_order = jnp.arange(tokens)
+    attended = head_block(
+        queries, key_rows, value_rows, segments, segments, token_order, token_order,
+        1.0 / math.sqrt(HD),
+    ).reshape(tokens, head_dev * HD)
+    terms = jnp.dot(attended, w_out[0], preferred_element_type=jnp.float32).astype(jnp.bfloat16)
+
+    gates = all_gates.transpose(1, 0, 2).reshape(local_experts, tokens)
+    member = gates > 0
+    before = (token_order[:, None] < token_order[None, :]).astype(jnp.bfloat16)
+    rank = jnp.dot(member.astype(jnp.bfloat16), before, preferred_element_type=jnp.float32)
+    slots = GROUP * CAP
+    slot_of = jnp.where(member, rank.astype(jnp.int32), -1)
+    places = jnp.arange(slots, dtype=jnp.int32)
+    chosen = slot_of[:, None, :] == places[None, :, None]
+    slot_gates = jnp.sum(jnp.where(chosen, gates[:, None, :], 0.0), axis=2, keepdims=True)
+    chosen = chosen.astype(jnp.bfloat16)
+    chosen_t = (slot_of.T[:, :, None] == places[None, None, :]).astype(jnp.bfloat16)
+    chosen_t = chosen_t.reshape(GROUP, tok_rows, local_experts * slots)
+
+    columns = width // CHUNKS
+    ff = w_down.shape[2]
+    vmem = pltpu.VMEM
+    in_place = pl.BlockSpec(memory_space=pl.ANY)
+    handed = pl.pallas_call(
+        closing_kernel,
+        out_shape=jax.ShapeDtypeStruct((tok_rows, width), jnp.bfloat16),
+        in_specs=[in_place] + in_vmem(5) + [in_place] * 2,
+        out_specs=pl.BlockSpec(memory_space=vmem),
+        scratch_shapes=[
+            vmem(w_gate_up.shape[1:], jnp.bfloat16),
+            vmem((2, local_experts, ff, columns), jnp.bfloat16),
+            vmem((CHUNKS, GROUP, tok_rows, columns), jnp.bfloat16),
+            vmem((CHUNKS, GROUP, tok_rows, columns), jnp.bfloat16),
+            vmem((CHUNKS, tok_rows, columns), jnp.bfloat16),
+            vmem((local_experts, slots, 2 * ff), jnp.float32),
+            vmem((local_experts, slots, ff), jnp.bfloat16),
+            vmem((local_experts * slots, columns), jnp.bfloat16),
+            vmem((CHUNKS, tok_rows, columns), jnp.float32),
+            vmem((tok_rows, width), jnp.bfloat16),
+        ]
+        + scatter_scratch(tok_rows, columns)
+        + scatter_scratch(tok_rows, columns)
+        + [
+            dma((CHUNKS, GROUP, 3)), dma((CHUNKS, GROUP)), dma((CHUNKS,)), dma((CHUNKS,)),
+            dma((2,)), dma((CHUNKS,)), dma((CHUNKS,)),
+        ],
+        compiler_params=remote_params(1, 60),
+    )(
+        terms.reshape(GROUP, tok_rows, width), acts[0], gains, chosen, chosen_t, slot_gates,
+        w_gate_up[0], w_down[0],
+    )
+    return handed[None]
+
+
 def solution(mesh):
     placed = (
         P("section", "expert", None),
@@ -194,7 +684,7 @@
         P("section", None),
     )
     return jax.shard_map(
-        per_device,
+        per_device if mesh.shape["expert"] == GROUP else per_device_general,
         mesh=mesh,
         in_specs=placed,
         out_specs=P("section", "expert", None),

time: 407 us -> 208 us (0.51)
  waiting for transfers between devices: 255 us -> 0 us
  Pallas kernels: 0 us -> 187 us
  blocking collectives: 72.9 us -> 0 us
  matrix products: 26 us -> 4.49 us
  between operations: 13.3 us -> 0.13 us
  local copies, waits for them, and re-layouts: 18 us -> 9.27 us
  starting transfers between devices: 7.19 us -> 0 us
  other arithmetic: 9.89 us -> 5.36 us
    pallas_call x0 -> x2, Pallas kernels: none -> 187 us  [the longest x1 148 us: per_device(): pl.pallas_call(closing_kernel, out_shape=jax.ShapeDtypeStruct((tok_rows,...]
    all_gather x2 -> x0, waiting for transfers between devices: 118 us -> none  [the longest x1 70.7 us: per_device(): gathered_keyval = lax.all_gather(w_keyval[0], 'expert', axis=0, tiled=True)]
    all_to_all x1 -> x0, blocking collectives: 72.9 us -> none  [per_device(): lax.all_to_all(send_rows, 'expert', split_axis=0, concat_axis=0, tiled=True)]
    all_to_all x1 -> x0, waiting for transfers between devices: 68.9 us -> none  [send_back(): lax.all_to_all(results, 'expert', split_axis=0, concat_axis=0, tiled=True)]
    reduce_scatter x1 -> x0, waiting for transfers between devices: 64.2 us -> none  [per_device(): lax.psum_scatter(jnp.dot(attended, out_weight, preferred_element_type=jnp...]
    dot_general x5 -> x4, matrix products: 25.6 us -> 4.11 us  [the longest x1 2.36 us: per_device(): jnp.dot(attended, w_out[0], preferred_element_type=jnp.float32)]
    gather x1 -> x0, local copies, waits for them, and re-layouts: 6.77 us -> none  [per_device(): returned.reshape(EXPERTS * CAP, width)[slot_index].astype(jnp.float32)]
    all_to_all x1 -> x0, starting transfers between devices: 5.49 us -> none  [send_back(): lax.all_to_all(results, 'expert', split_axis=0, concat_axis=0, tiled=True)]
  transfers between devices with their start and end apart: 5 -> 0, of which waited for: 5 -> 0; matrix products, arithmetic and copies ran while one was open for 2% -> 0% of each run, Pallas kernels for 0% -> 0%
where the time goes in v2:
time: 208 us; the launch traced here: 206 us
  Pallas kernels  187 us (90%)
  local copies, waits for them, and re-layouts  9.27 us (4%)
  other arithmetic  5.36 us (3%)
  matrix products  4.49 us (2%)
    pallas_call x1, Pallas kernels, per_device(): pl.pallas_call(closing_kernel, out_shape=jax.ShapeDtypeStruct((tok_rows,...  148 us
    pallas_call x1, Pallas kernels, per_device(): pl.pallas_call(opening_kernel, out_shape=[jax.ShapeDtypeStruct((1, GROUP,...  38.7 us
    unnamed x12, local copies, waits for them, and re-layouts  4.75 us

profile of v2, /device:TPU:9, one launch (start us, length us, event | category | flops | bytes accessed | tf_op | source)
XLA Modules:
  0.0 206.3 jit_solution(17072989605621425515)
XLA Ops:
  0.0 0.0 copy-start
  0.0 1.2 copy.26
  1.2 0.7 select_reduce_fusion.1
  1.9 0.0 copy-start.1
  1.9 0.9 copy-done.1
  2.9 0.0 copy-start.2
  2.9 0.7 copy-done.2
  3.6 38.7 %shard_map.103 = (bf16[1,8,64,2048]{3,2,1,0:T(8,128)(2,1)S(1)}, bf16[8,256,256]{2,1,0:T(8,128)(2,1)S(1)}, f32[8,4,64]{2,1,0:T(4,128)S(1)}) custom-call(bf16[64,2048]{1,0:T(8,128)(2,1)S(1)} %bitcast.65, f32[2,2048]{1,0:T(2,128)S(1)} %bitcast.67, bf16[4,256,256]{2,1,0:T(8,128)(2,1)S(1)} %bitcast.63, f32[8,4,64]{2,1,0:T(4,128)S(1)} %bitcast.68), custom_call_target="tpu_custom_call" | custom-call | tf_op jit(solution)/shard_map/pallas_call | solution.py:593
  42.3 0.0 copy-start.3
  42.3 0.8 fusion.44
  43.1 0.0 copy-start.4
  43.1 0.2 copy-done.3
  43.4 0.8 convolution_bitcast_fusion
  44.2 0.6 fusion.36
  44.8 0.0 copy-done.4
  44.9 0.4 fusion.43
  45.2 0.2 fusion.6
  45.4 0.0 copy-done
  45.4 2.4 %convolution_convert_fusion = bf16[512,2048]{1,0:T(8,128)(2,1)} fusion(bf16[1,128,2048]{2,1,0:T(8,128)(2,1)S(1)} %copy-done, f32[1,512,512]{1,2,0:T(8,128)S(1)} %get-tuple-element.18, f32[512]{0:T(512)S(1)} %fusion.6, f32[512]{0:T(512)S(1)} %get-tuple-element.17, f32[512,256]{0,1:T(8,128)S(1)} %fusion.44), kind=kOutput, calls=%fused_computation | convolution fusion | flops 337444864 | bytes 3805184 | tf_op jit(solution)/shard_map/dot_general | solution.py:623
  47.8 0.1 reshape.244
  47.9 0.2 fusion.4
  48.1 0.3 select_reduce_fusion
  48.3 1.0 copy.24.slot_gates
  49.3 0.1 copy.23
  49.4 0.7 eq.78
  50.1 2.5 %eq.79 = s32[8,64,768]{2,1,0:T(8,128)} reshape(s32[512,4,192]{2,1,0:T(4,128)S(1)} %eq.78) | data formatting | bytes 3145728 | tf_op jit(solution)/shard_map/eq | solution.py:635
  52.7 0.1 eq.81
  52.7 2.4 %compare_convert_fusion.chosen_t = bf16[8,64,768]{2,1,0:T(8,128)(2,1)} fusion(s32[8,64,768]{2,1,0:T(8,128)} %eq.79, s32[768]{0:T(1024)S(1)} %eq.81), kind=kLoop, calls=%fused_computation.4 | loop fusion | flops 786432 | bytes 2362368 | tf_op jit(solution)/shard_map/convert_element_type | solution.py:635
  55.2 1.1 fusion.chosen
  56.3 148.3 %shard_map.104 = bf16[64,2048]{1,0:T(8,128)(2,1)} custom-call(bf16[8,64,2048]{2,1,0:T(8,128)(2,1)} %bitcast.73, bf16[64,2048]{1,0:T(8,128)(2,1)} %bitcast.64, f32[2,2048]{1,0:T(2,128)} %bitcast.66, bf16[4,192,512]{2,1,0:T(8,128)(2,1)} %fusion.chosen, bf16[8,64,768]{2,1,0:T(8,128)(2,1)} %compare_convert_fusion.chosen_t, f32[4,192,1]{2,1,0:T(8,128)} %copy.24.slot_gates, ...), custom_call_target="tpu_custom_call" | custom-call | tf_op jit(solution)/shard_map/pallas_call | solution.py:642
  204.6 1.7 copy.28
  (5 shorter events, 0.0 us)
Async XLA Ops:
  0.0 45.4 %copy-start = (bf16[1,128,2048]{2,1,0:T(8,128)(2,1)S(1)}, bf16[1,128,2048]{2,1,0:T(8,128)(2,1)}, u32[]{:S(2)}) copy-start(bf16[1,128,2048]{2,1,0:T(8,128)(2,1)} %param.14) | copy-start | bytes 1572868
  1.9 1.0 copy-start.1
  2.9 0.7 copy-start.2
  42.3 1.0 copy-start.3
  43.1 1.7 copy-start.4

commit v3 on v1

--- a/solution.py
+++ b/solution.py
@@ -318,55 +318,153 @@
     return [slots] * 4 + [sems] * 5 + [pltpu.VMEM((rows, width), jnp.float32)]
 
 
-def opening_kernel(acts, gains, keyval, routes, rows, weights, all_routes,
-                   send_sems, recv_sems, keyval_send, keyval_recv, route_send, route_recv,
-                   local_sem):
+def remote(src, dst, send_sem, recv_sem, expert, section=None):
+    if section is None:
+        section = lax.axis_index("section")
+    return pltpu.make_async_remote_copy(
+        src_ref=src,
+        dst_ref=dst,
+        send_sem=send_sem,
+        recv_sem=recv_sem,
+        device_id=(section, expert),
+        device_id_type=MESH,
+    )
+
+
+def at_place(body):
+    me = lax.axis_index("expert")
+    x = lax.rem(me, 2)
+    for z in range(LINE):
+
+        @pl.when(me // 2 == z)
+        def _(z=z):
+            body(z, x, z * 2 + x, z * 2 + 1 - x)
+
+
+class Gather:
+    def __init__(self, rows, send_sems, recv_sems):
+        self.rows, self.send_sems, self.recv_sems = rows, send_sems, recv_sems
+
+    def copy(self, chunk, shard, to, way):
+        return remote(
+            self.rows.at[chunk, shard], self.rows.at[chunk, shard],
+            self.send_sems.at[chunk, shard, way], self.recv_sems.at[chunk, shard], to,
+        )
+
+    def first(self, chunk, z, own, partner):
+        out = []
+        if z < LINE - 1:
+            out.append(self.copy(chunk, own, own + 2, 0))
+        if z > 0:
+            out.append(self.copy(chunk, own, own - 2, 1))
+        return out + [self.copy(chunk, own, partner, 2)]
+
+    def passing(self, chunk, z, x, own, partner):
+        out = []
+        for far in range(1, LINE):
+            if z - far >= 0:
+                shard = (z - far) * 2 + x
+                onward = [self.copy(chunk, shard, own + 2, 0)] if z < LINE - 1 else []
+                out.append((shard, onward + [self.copy(chunk, shard, partner, 2)]))
+            if z + far < LINE:
+                shard = (z + far) * 2 + x
+                onward = [self.copy(chunk, shard, own - 2, 1)] if z > 0 else []
+                out.append((shard, onward + [self.copy(chunk, shard, partner, 2)]))
+        return out
+
+    def start(self, chunk, z, x, own, partner):
+        for out in self.first(chunk, z, own, partner):
+            out.start()
+
+    def forward(self, chunk, z, x, own, partner):
+        for shard, onward in self.passing(chunk, z, x, own, partner):
+            self.copy(chunk, shard, partner, 2).wait_recv()
+            for out in onward:
+                out.start()
+
+    def arrive(self, chunk, z, x, own, partner):
+        for place in range(LINE):
+            self.copy(chunk, place * 2 + 1 - x, partner, 2).wait_recv()
+
+    def drain(self, chunk, z, x, own, partner):
+        for out in self.first(chunk, z, own, partner):
+            out.wait_send()
+        for _, onward in self.passing(chunk, z, x, own, partner):
+            for out in onward:
+                out.wait_send()
+
+
+def opening_kernel(acts, gains, keyval, gates, rows, weights, all_gates,
+                   send_sems, recv_sems, keyval_send, keyval_recv, pass_send, gate_send,
+                   gate_recv, local_sem):
     section, me = lax.axis_index("section"), lax.axis_index("expert")
-    rows[me] = rms_scale(acts[...].astype(jnp.float32), gains[0:1, :]).astype(jnp.bfloat16)
+    rows[0, me] = rms_scale(acts[...].astype(jnp.float32), gains[0:1, :]).astype(jnp.bfloat16)
     greet(False)
-    place = me // 2
-    own_weights = pltpu.make_async_copy(keyval.at[place], weights.at[me], local_sem.at[0])
-    own_routes = pltpu.make_async_copy(routes, all_routes.at[me], local_sem.at[1])
-
-    def side_copies():
-        keyval_copies, route_copies = [], []
-        for step in range(1, GROUP):
-            other = lax.rem(me + step, GROUP)
-            keyval_copies.append(pltpu.make_async_remote_copy(
-                src_ref=keyval.at[other // 2],
-                dst_ref=weights.at[me],
-                send_sem=keyval_send.at[step],
-                recv_sem=keyval_recv.at[step],
-                device_id=(section, other),
-                device_id_type=MESH,
-            ))
-            route_copies.append(pltpu.make_async_remote_copy(
-                src_ref=routes,
-                dst_ref=all_routes.at[me],
-                send_sem=route_send.at[step],
-                recv_sem=route_recv.at[step],
-                device_id=(section, other),
-                device_id_type=MESH,
-            ))
-        return keyval_copies + route_copies
-
-    side = side_copies()
+    gather = Gather(rows, send_sems, recv_sems)
+    own_gates = pltpu.make_async_copy(gates.at[me], all_gates.at[me], local_sem.at[1])
+    own_weights = pltpu.make_async_copy(keyval.at[me // 2], weights.at[me], local_sem.at[0])
+    gate_copies = []
+    for step in range(1, GROUP):
+        other = lax.rem(me + step, GROUP)
+        gate_copies.append(
+            remote(gates.at[other], all_gates.at[me], gate_send.at[step], gate_recv.at[step], other)
+        )
+
+    def line_weights(place, z, own):
+        return remote(
+            keyval.at[place], weights.at[own], keyval_send.at[place], keyval_recv.at[own],
+            own + 2 * (place - z),
+        )
+
+    def pass_weights(place, z, x, partner):
+        shard = place * 2 + x
+        source = keyval.at[z] if place == z else weights.at[shard]
+        return remote(source, weights.at[shard], pass_send.at[place], keyval_recv.at[shard], partner)
+
+    def begin(z, x, own, partner):
+        gather.start(0, z, x, own, partner)
+        for place in LINE_ORDER[z]:
+            if place != z:
+                line_weights(place, z, own).start()
+        pass_weights(z, z, x, partner).start()
+
+    def through(z, x, own, partner):
+        nearest = sorted((p for p in range(LINE) if p != z), key=lambda p: abs(p - z))
+        for place, (shard, onward) in zip(nearest, gather.passing(0, z, x, own, partner)):
+            gather.copy(0, shard, partner, 2).wait_recv()
+            for out in onward:
+                out.start()
+            source = place * 2 + x
+            remote(
+                weights.at[source], weights.at[source], pass_send.at[place],
+                keyval_recv.at[source], partner,
+            ).wait_recv()
+            pass_weights(place, z, x, partner).start()
+        gather.arrive(0, z, x, own, partner)
+        for place in range(LINE):
+            source = place * 2 + 1 - x
+            remote(
+                weights.at[source], weights.at[source], pass_send.at[place],
+                keyval_recv.at[source], partner,
+            ).wait_recv()
+        gather.drain(0, z, x, own, partner)
+        for place in range(LINE):
+            if place != z:
+                line_weights(place, z, own).wait_send()
+            pass_weights(place, z, x, partner).wait_send()
+
+    at_place(begin)
     own_weights.start()
-    own_routes.start()
-    for out in side:
+    own_gates.start()
+    for out in gate_copies:
         out.start()
-    for z in range(LINE):
-
-        @pl.when(place == z)
-        def _(z=z):
-            gather_line(z, rows, send_sems, recv_sems)()
-
-    for out in side:
+    at_place(through)
+    for out in gate_copies:
         out.wait_recv()
-    for out in side:
+    for out in gate_copies:
         out.wait_send()
     own_weights.wait()
-    own_routes.wait()
+    own_gates.wait()
 
 
 def turning_kernel(terms, acts, gains, rows, middle,
@@ -415,9 +513,9 @@
     return [pl.BlockSpec(memory_space=pltpu.VMEM)] * count
 
 
-def remote_params(collective_id):
+def remote_params(collective_id, mebibytes):
     return pltpu.CompilerParams(
-        collective_id=collective_id, has_side_effects=True, vmem_limit_bytes=40 << 20
+        collective_id=collective_id, has_side_effects=True, vmem_limit_bytes=mebibytes << 20
     )
 
 
@@ -433,7 +531,6 @@
     gate_weights,
     segment_ids,
 ):
-    my_index = lax.axis_index("expert")
     tok_rows, width = acts.shape[1:]
     head_dev = w_query.shape[2] // HD
     local_experts = w_gate_up.shape[1]
@@ -441,26 +538,25 @@
     tokens = tok_rows * GROUP
     keyval = w_keyval[0].transpose(1, 0, 2)
     keyval_rows = keyval.shape[1]
-    pairs = tok_rows * TOPK
-    routes = jnp.concatenate(
-        [expert_ids[0].astype(jnp.float32).reshape(-1, 128), gate_weights[0].reshape(-1, 128)]
-    )
+    named = expert_ids[0][:, :, None] == jnp.arange(EXPERTS, dtype=jnp.int32)[None, None, :]
+    dense_gates = jnp.sum(jnp.where(named, gate_weights[0][:, :, None], 0.0), axis=1)
+    dense_gates = dense_gates.T.reshape(GROUP, local_experts, tok_rows)
     dma = pltpu.SemaphoreType.DMA
-    row_piece, head_keyval, all_routes = pl.pallas_call(
+    row_piece, head_keyval, all_gates = pl.pallas_call(
         opening_kernel,
         out_shape=[
-            jax.ShapeDtypeStruct((GROUP, tok_rows, width), jnp.bfloat16),
+            jax.ShapeDtypeStruct((1, GROUP, tok_rows, width), jnp.bfloat16),
             jax.ShapeDtypeStruct((GROUP, keyval_rows, 2 * HD), jnp.bfloat16),
-            jax.ShapeDtypeStruct((GROUP,) + routes.shape, jnp.float32),
+            jax.ShapeDtypeStruct(dense_gates.shape, jnp.float32),
         ],
         in_specs=in_vmem(4),
         out_specs=in_vmem(3),
         scratch_shapes=[
-            dma((GROUP, 3)), dma((GROUP,)), dma((GROUP,)), dma((GROUP,)), dma((GROUP,)),
-            dma((GROUP,)), dma((2,)),
+            dma((1, GROUP, 3)), dma((1, GROUP)), dma((LINE,)), dma((GROUP,)), dma((LINE,)),
+            dma((GROUP,)), dma((GROUP,)), dma((2,)),
         ],
-        compiler_params=remote_params(0),
-    )(acts[0], gains, keyval, routes)
+        compiler_params=remote_params(0, 8),
+    )(acts[0], gains, keyval, dense_gates)
     row_piece = row_piece.reshape(tokens, width)
     head_keyval = head_keyval.reshape(width, 2 * HD)
 
@@ -486,23 +582,19 @@
         in_specs=in_vmem(3),
         out_specs=in_vmem(2),
         scratch_shapes=scatter_scratch(tok_rows, width) + [dma((GROUP, 3)), dma((GROUP,))],
-        compiler_params=remote_params(1),
+        compiler_params=remote_params(1, 12),
     )(terms.reshape(GROUP, tok_rows, width), acts[0], gains)
     mixer_rows = mixer_rows.reshape(tokens, width)
 
-    lines = pairs // 128
-    all_ids = all_routes[:, :lines].reshape(tokens, TOPK).astype(jnp.int32)
-    all_gates = all_routes[:, lines:].reshape(tokens, TOPK)
-    experts_here = my_index * local_experts + jnp.arange(local_experts, dtype=jnp.int32)
-    named = all_ids[:, :, None] == experts_here[None, None, :]
-    gates = jnp.sum(jnp.where(named, all_gates[:, :, None], 0.0), axis=1)
-    member = jnp.any(named, axis=1)
-    before = (token_order[:, None] > token_order[None, :]).astype(jnp.bfloat16)
-    rank = jnp.dot(before, member.astype(jnp.bfloat16), preferred_element_type=jnp.float32)
+    gates = all_gates.transpose(1, 0, 2).reshape(local_experts, tokens)
+    member = gates > 0
+    before = (token_order[:, None] < token_order[None, :]).astype(jnp.bfloat16)
+    rank = jnp.dot(member.astype(jnp.bfloat16), before, preferred_element_type=jnp.float32)
     slots = GROUP * CAP
-    slot_of = jnp.where(member, rank.astype(jnp.int32), -1).T
-    chosen = slot_of[:, None, :] == jnp.arange(slots, dtype=jnp.int32)[None, :, None]
-    slot_gates = jnp.sum(jnp.where(chosen, gates.T[:, None, :], 0.0), axis=2)
+    slot_of = jnp.where(member, rank.astype(jnp.int32), -1)
+    places = jnp.arange(slots, dtype=jnp.int32)
+    chosen = slot_of[:, None, :] == places[None, :, None]
+    slot_gates = jnp.sum(jnp.where(chosen, gates[:, None, :], 0.0), axis=2)
     chosen = chosen.astype(jnp.bfloat16)
     grouped = jnp.einsum(
         "est,td->esd", chosen, mixer_rows, preferred_element_type=jnp.float32
@@ -527,7 +619,7 @@
         out_specs=pl.BlockSpec(memory_space=pltpu.VMEM),
         scratch_shapes=scatter_scratch(tok_rows, width)
         + [pltpu.VMEM((tok_rows, width), jnp.bfloat16), dma, dma],
-        compiler_params=remote_params(2),
+        compiler_params=remote_params(2, 10),
     )(mixed.reshape(GROUP, tok_rows, width), middle)
     return handed[None]
 

time: 186 us -> 170 us (0.914)
  Pallas kernels: 146 us -> 131 us
    pallas_call x1, Pallas kernels: 57.5 us -> 48.8 us  [per_device(): pl.pallas_call(turning_kernel, out_shape=[jax.ShapeDtypeStruct((GROUP, to...]
    pallas_call x1, Pallas kernels: 45.3 us -> 38.7 us  [per_device(): pl.pallas_call(opening_kernel, out_shape=[jax.ShapeDtypeStruct((1, GROUP,...]
    unnamed x23 -> x22, local copies, waits for them, and re-layouts: 6.63 us -> 5.84 us
where the time goes in v3:
time: 170 us
  Pallas kernels  131 us (77%)
  matrix products  30.5 us (18%)
  local copies, waits for them, and re-layouts  5.94 us (3%)
  other arithmetic  1.84 us (1%)
    pallas_call x1, Pallas kernels, per_device(): pl.pallas_call(turning_kernel, out_shape=[jax.ShapeDtypeStruct((GROUP, to...  48.8 us
    pallas_call x1, Pallas kernels, per_device(): pl.pallas_call(closing_kernel, out_shape=jax.ShapeDtypeStruct((tok_rows,...  43.7 us
    pallas_call x1, Pallas kernels, per_device(): pl.pallas_call(opening_kernel, out_shape=[jax.ShapeDtypeStruct((1, GROUP,...  38.7 us
    dot_general x1, matrix products, per_device(): jnp.einsum('esd,edf->esf', grouped, w_gate_up[0], preferred_element_type=...  15.2 us
    dot_general x1, matrix products, per_device(): jnp.dot(chosen.reshape(local_experts * slots, tokens).T, outputs.reshape(...  10.8 us
    unnamed x22, local copies, waits for them, and re-layouts  5.84 us

profile of v3, /device:TPU:9, one launch (start us, length us, event | category | flops | bytes accessed | tf_op | source)
XLA Modules:
  0.0 169.7 jit_solution(6957652135757300099)
XLA Ops:
  0.0 0.0 copy-start
  0.0 0.8 select_reduce_fusion.1
  0.8 1.1 copy.21
  1.9 0.0 copy-start.1
  1.9 0.9 copy-done.1
  2.9 0.0 copy-start.3
  2.9 0.7 copy-done.3
  3.6 0.0 copy-start.7
  3.6 38.7 %shard_map.103 = (bf16[1,8,64,2048]{3,2,1,0:T(8,128)(2,1)S(1)}, bf16[8,256,256]{2,1,0:T(8,128)(2,1)S(1)}, f32[8,4,64]{2,1,0:T(4,128)S(1)}) custom-call(bf16[64,2048]{1,0:T(8,128)(2,1)S(1)} %bitcast.79, f32[2,2048]{1,0:T(2,128)S(1)} %bitcast.82, bf16[4,256,256]{2,1,0:T(8,128)(2,1)S(1)} %bitcast.78, f32[8,4,64]{2,1,0:T(4,128)S(1)} %bitcast.84), custom_call_target="tpu_custom_call" | custom-call | tf_op jit(solution)/shard_map/pallas_call | solution.py:545
  42.4 0.8 fusion.62
  43.1 0.0 copy-done.7
  43.1 0.0 copy-start.8
  43.1 0.0 copy-start.9
  43.1 0.8 convolution_bitcast_fusion
  44.0 0.1 reshape.243
  44.1 0.2 fusion.17
  44.2 0.3 select_reduce_fusion
  44.5 0.6 fusion.52
  45.1 0.0 copy-done.9
  45.1 0.4 fusion.61
  45.5 0.0 copy-done.8
  45.5 0.0 copy-start.6
  45.5 1.0 copy-done.6
  46.5 0.2 fusion.19
  46.7 0.0 copy-done
  46.7 0.0 copy-start.2
  46.7 0.0 copy-start.4
  46.7 2.3 %convolution_convert_fusion.1 = bf16[512,2048]{1,0:T(8,128)(2,1)S(1)} fusion(bf16[1,128,2048]{2,1,0:T(8,128)(2,1)S(1)} %copy-done, f32[1,512,512]{1,2,0:T(8,128)} %copy-done.6, f32[512]{0:T(512)S(1)} %fusion.19, f32[512]{0:T(512)S(1)} %get-tuple-element.21, f32[512,256]{0,1:T(8,128)} %copy-done.8), kind=kOutput, calls=%fused_computation.8 | convolution fusion | flops 337444864 | bytes 3805184 | tf_op jit(solution)/shard_map/dot_general | solution.py:575
  49.1 0.0 copy-done.2
  49.1 0.0 copy-done.4
  49.1 48.8 %shard_map.104 = (bf16[8,64,2048]{2,1,0:T(8,128)(2,1)S(1)}, bf16[64,2048]{1,0:T(8,128)(2,1)S(1)}) custom-call(bf16[8,64,2048]{2,1,0:T(8,128)(2,1)S(1)} %bitcast.75, bf16[64,2048]{1,0:T(8,128)(2,1)S(1)} %bitcast.80, f32[2,2048]{1,0:T(2,128)S(1)} %bitcast.83), custom_call_target="tpu_custom_call" | custom-call | tf_op jit(solution)/shard_map/pallas_call | solution.py:576
  97.9 0.0 copy-start.5
  97.9 1.4 copy-done.5
  99.3 15.2 %fusion = f32[4,192,1536]{2,1,0:T(8,128)} fusion(bf16[1,4,2048,1536]{3,2,1,0:T(8,128)(2,1)} %param.15, bf16[512,2048,1]{1,0,2:T(8,128)(2,1)} %bitcast.86, s32[4,512]{1,0:T(4,128)S(1)} %fusion.17), kind=kOutput, calls=%fused_computation | convolution fusion | flops 6444417024 | bytes 31989760 | tf_op jit(solution)/shard_map/esd,edf->esf/dot_general | solution.py:602
  114.5 10.8 %bitcast_convert_fusion = bf16[512,2048]{1,0:T(8,128)(2,1)S(1)} fusion(bf16[1,4,768,2048]{3,2,1,0:T(8,128)(2,1)} %param.16, f32[4,192]{1,0:T(4,128)S(1)} %select_reduce_fusion, f32[4,192,1536]{2,1,0:T(8,128)} %fusion, s32[4,512]{1,0:T(4,128)S(1)} %fusion.17), kind=kOutput, calls=%fused_computation.5 | convolution fusion | flops 4034658304 | bytes 19409920 | tf_op jit(solution)/shard_map/dot_general | solution.py:609
  125.3 43.7 %shard_map.105 = bf16[64,2048]{1,0:T(8,128)(2,1)S(1)} custom-call(bf16[8,64,2048]{2,1,0:T(8,128)(2,1)S(1)} %bitcast.74, bf16[64,2048]{1,0:T(8,128)(2,1)S(1)} %get-tuple-element.14.middle), custom_call_target="tpu_custom_call" | custom-call | tf_op jit(solution)/shard_map/pallas_call | solution.py:615
  169.0 0.7 copy.23
  (4 shorter events, 0.0 us)
Async XLA Ops:
  0.0 46.7 %copy-start = (bf16[1,128,2048]{2,1,0:T(8,128)(2,1)S(1)}, bf16[1,128,2048]{2,1,0:T(8,128)(2,1)}, u32[]{:S(2)}) copy-start(bf16[1,128,2048]{2,1,0:T(8,128)(2,1)} %param.14) | copy-start | bytes 1572868
  1.9 1.0 copy-start.1
  2.9 0.7 copy-start.3
  3.6 39.5 %copy-start.7 = (bf16[1,2048,128]{2,1,0:T(8,128)(2,1)S(1)}, bf16[1,2048,128]{2,1,0:T(8,128)(2,1)}, u32[]{:S(2)}) copy-start(bf16[1,2048,128]{2,1,0:T(8,128)(2,1)} %param.12) | copy-start | bytes 1572868
  43.1 2.4 %copy-start.8 = (f32[512,256]{0,1:T(8,128)}, f32[512,256]{0,1:T(8,128)S(1)}, u32[]{:S(2)}) copy-start(f32[512,256]{0,1:T(8,128)S(1)} %fusion.62) | copy-start | bytes 1572868
  43.1 2.0 %copy-start.9 = (s32[1,512]{1,0:T(1,128)S(1)}, s32[1,512]{1,0:T(1,128)}, u32[]{:S(2)}) copy-start(s32[1,512]{1,0:T(1,128)} %param.19) | copy-start | bytes 6148
  45.5 1.0 copy-start.6
  46.7 2.4 %copy-start.2 = (bf16[1,64,2048]{2,1,0:T(8,128)(2,1)S(1)}, bf16[1,64,2048]{2,1,0:T(8,128)(2,1)}, u32[]{:S(2)}) copy-start(bf16[1,64,2048]{2,1,0:T(8,128)(2,1)} %param.10) | copy-start | bytes 786436
  46.7 2.4 %copy-start.4 = (f32[1,2,2048]{2,1,0:T(2,128)S(1)}, f32[1,2,2048]{2,1,0:T(2,128)}, u32[]{:S(2)}) copy-start(f32[1,2,2048]{2,1,0:T(2,128)} %param.11) | copy-start | bytes 49156
  97.9 1.4 copy-start.5

commit v4 on v3

--- a/solution.py
+++ b/solution.py
@@ -186,6 +186,7 @@
 
 LINE = 4
 GROUP = 8
+PARTS = 2
 
 
 def greet(section_too):
@@ -204,118 +205,60 @@
     pl.semaphore_wait(barrier, count)
 
 
-def gather_line(z, rows, send_sems, recv_sems):
-    section, me = lax.axis_index("section"), lax.axis_index("expert")
-    x = lax.rem(me, 2)
-    partner = z * 2 + 1 - x
-
-    def copy(shard, to, way):
-        return pltpu.make_async_remote_copy(
-            src_ref=rows.at[shard],
-            dst_ref=rows.at[shard],
-            send_sem=send_sems.at[shard, way],
-            recv_sem=recv_sems.at[shard],
-            device_id=(section, to),
-            device_id_type=MESH,
-        )
-
-    sent = []
-
-    def send(shard, to, way):
-        out = copy(shard, to, way)
-        out.start()
-        sent.append(out)
-
-    own = z * 2 + x
-    if z < LINE - 1:
-        send(own, own + 2, 0)
-    if z > 0:
-        send(own, own - 2, 1)
-    send(own, partner, 2)
-    for far in range(1, LINE):
-        if z - far >= 0:
-            shard = (z - far) * 2 + x
-            copy(shard, partner, 2).wait_recv()
-            if z < LINE - 1:
-                send(shard, own + 2, 0)
-            send(shard, partner, 2)
-        if z + far < LINE:
-            shard = (z + far) * 2 + x
-            copy(shard, partner, 2).wait_recv()
-            if z > 0:
-                send(shard, own - 2, 1)
-            send(shard, partner, 2)
-
-    def finish():
-        for place in range(LINE):
-            copy(place * 2 + 1 - x, partner, 2).wait_recv()
-        for out in sent:
-            out.wait_send()
-
-    return finish
-
-
 LINE_ORDER = ((3, 2, 1, 0), (3, 0, 2, 1), (0, 3, 1, 2), (0, 1, 2, 3))
 
 
 def scatter_line(z, terms, from_pair, from_below, from_above, outgoing, pair_send, pair_recv,
-                 line_send, below_recv, above_recv, total):
+                 line_send, below_recv, above_recv, ready):
     section, me = lax.axis_index("section"), lax.axis_index("expert")
     x = lax.rem(me, 2)
     own = z * 2 + x
     partner = z * 2 + 1 - x
-    pair_copies = {}
-    for place in LINE_ORDER[z]:
-        pair_copies[place] = pltpu.make_async_remote_copy(
-            src_ref=terms.at[place * 2 + 1 - x],
-            dst_ref=from_pair.at[place],
-            send_sem=pair_send.at[place],
-            recv_sem=pair_recv.at[place],
-            device_id=(section, partner),
-            device_id_type=MESH,
-        )
-        pair_copies[place].start()
-
-    def line_copy(place, up):
-        return pltpu.make_async_remote_copy(
-            src_ref=outgoing.at[place],
-            dst_ref=(from_below if up else from_above).at[place],
-            send_sem=line_send.at[place],
-            recv_sem=(below_recv if up else above_recv).at[place],
-            device_id=(section, own + 2 if up else own - 2),
-            device_id_type=MESH,
+    order = [(place, part) for place in LINE_ORDER[z] for part in range(PARTS)]
+    pair_copies = {
+        (place, part): remote(
+            terms.at[place * 2 + 1 - x, part], from_pair.at[place, part],
+            pair_send.at[place, part], pair_recv.at[place, part], partner,
+        )
+        for place, part in order
+    }
+    for item in order:
+        pair_copies[item].start()
+
+    def line_copy(place, part, up):
+        landing, sems = (from_below, below_recv) if up else (from_above, above_recv)
+        return remote(
+            outgoing.at[place, part], landing.at[place, part], line_send.at[place, part],
+            sems.at[place, part], own + 2 if up else own - 2,
         )
 
     sent = []
-    for place in LINE_ORDER[z]:
-        pair_copies[place].wait_recv()
-        parts = [terms.at[place * 2 + x], from_pair.at[place]]
+    for place, part in order:
+        pair_copies[place, part].wait_recv()
+        pieces = [from_pair.at[place, part]]
         if place >= z and z > 0:
-            line_copy(place, True).wait_recv()
-            parts.append(from_below.at[place])
+            line_copy(place, part, True).wait_recv()
+            pieces.append(from_below.at[place, part])
         if place <= z and z < LINE - 1:
-            line_copy(place, False).wait_recv()
-            parts.append(from_above.at[place])
-        value = parts[0][...].astype(jnp.float32)
-        for part in parts[1:]:
-            value = value + part[...].astype(jnp.float32)
+            line_copy(place, part, False).wait_recv()
+            pieces.append(from_above.at[place, part])
+        value = terms[place * 2 + x, part].astype(jnp.float32)
+        for piece in pieces:
+            value = value + piece[...].astype(jnp.float32)
         if place == z:
-            total[...] = value
+            ready(part, value)
         else:
-            outgoing[place] = value.astype(jnp.bfloat16)
-            out = line_copy(place, place > z)
+            outgoing[place, part] = value.astype(jnp.bfloat16)
+            out = line_copy(place, part, place > z)
             out.start()
             sent.append(out)
-    for place in range(LINE):
-        pair_copies[place].wait_send()
-    for out in sent:
-        out.wait_send()
+    return list(pair_copies.values()) + sent
 
 
 def scatter_scratch(rows, width):
-    slots = pltpu.VMEM((LINE, rows, width), jnp.bfloat16)
-    sems = pltpu.SemaphoreType.DMA((LINE,))
-    return [slots] * 4 + [sems] * 5 + [pltpu.VMEM((rows, width), jnp.float32)]
+    slots = pltpu.VMEM((LINE, PARTS, rows // PARTS, width), jnp.bfloat16)
+    sems = pltpu.SemaphoreType.DMA((LINE, PARTS))
+    return [slots] * 4 + [sems] * 5
 
 
 def remote(src, dst, send_sem, recv_sem, expert, section=None):
@@ -347,7 +290,7 @@
 
     def copy(self, chunk, shard, to, way):
         return remote(
-            self.rows.at[chunk, shard], self.rows.at[chunk, shard],
+            self.rows.at[shard, chunk], self.rows.at[shard, chunk],
             self.send_sems.at[chunk, shard, way], self.recv_sems.at[chunk, shard], to,
         )
 
@@ -398,7 +341,10 @@
                    send_sems, recv_sems, keyval_send, keyval_recv, pass_send, gate_send,
                    gate_recv, local_sem):
     section, me = lax.axis_index("section"), lax.axis_index("expert")
-    rows[0, me] = rms_scale(acts[...].astype(jnp.float32), gains[0:1, :]).astype(jnp.bfloat16)
+    for part in range(PARTS):
+        rows[me, part] = rms_scale(acts[part].astype(jnp.float32), gains[0:1, :]).astype(
+            jnp.bfloat16
+        )
     greet(False)
     gather = Gather(rows, send_sems, recv_sems)
     own_gates = pltpu.make_async_copy(gates.at[me], all_gates.at[me], local_sem.at[1])
@@ -422,7 +368,8 @@
         return remote(source, weights.at[shard], pass_send.at[place], keyval_recv.at[shard], partner)
 
     def begin(z, x, own, partner):
-        gather.start(0, z, x, own, partner)
+        for part in range(PARTS):
+            gather.start(part, z, x, own, partner)
         for place in LINE_ORDER[z]:
             if place != z:
                 line_weights(place, z, own).start()
@@ -430,24 +377,28 @@
 
     def through(z, x, own, partner):
         nearest = sorted((p for p in range(LINE) if p != z), key=lambda p: abs(p - z))
-        for place, (shard, onward) in zip(nearest, gather.passing(0, z, x, own, partner)):
-            gather.copy(0, shard, partner, 2).wait_recv()
-            for out in onward:
-                out.start()
+        hops = [gather.passing(part, z, x, own, partner) for part in range(PARTS)]
+        for place, *arrivals in zip(nearest, *hops):
+            for part, (shard, onward) in enumerate(arrivals):
+                gather.copy(part, shard, partner, 2).wait_recv()
+                for out in onward:
+                    out.start()
             source = place * 2 + x
             remote(
                 weights.at[source], weights.at[source], pass_send.at[place],
                 keyval_recv.at[source], partner,
             ).wait_recv()
             pass_weights(place, z, x, partner).start()
-        gather.arrive(0, z, x, own, partner)
+        for part in range(PARTS):
+            gather.arrive(part, z, x, own, partner)
         for place in range(LINE):
             source = place * 2 + 1 - x
             remote(
                 weights.at[source], weights.at[source], pass_send.at[place],
                 keyval_recv.at[source], partner,
             ).wait_recv()
-        gather.drain(0, z, x, own, partner)
+        for part in range(PARTS):
+            gather.drain(part, z, x, own, partner)
         for place in range(LINE):
             if place != z:
                 line_weights(place, z, own).wait_send()
@@ -469,44 +420,62 @@
 
 def turning_kernel(terms, acts, gains, rows, middle,
                    from_pair, from_below, from_above, outgoing, pair_send, pair_recv,
-                   line_send, below_recv, above_recv, total, send_sems, recv_sems):
+                   line_send, below_recv, above_recv, send_sems, recv_sems):
     me = lax.axis_index("expert")
     greet(False)
-    for z in range(LINE):
-
-        @pl.when(me // 2 == z)
-        def _(z=z):
-            scatter_line(z, terms, from_pair, from_below, from_above, outgoing, pair_send,
-                         pair_recv, line_send, below_recv, above_recv, total)
-            joined = (acts[...].astype(jnp.float32) + total[...]).astype(jnp.bfloat16)
-            middle[...] = joined
-            rows[me] = rms_scale(joined.astype(jnp.float32), gains[1:2, :]).astype(jnp.bfloat16)
-            gather_line(z, rows, send_sems, recv_sems)()
+    gather = Gather(rows, send_sems, recv_sems)
+
+    def body(z, x, own, partner):
+        def ready(part, total):
+            joined = (acts[part].astype(jnp.float32) + total).astype(jnp.bfloat16)
+            middle[part] = joined
+            rows[me, part] = rms_scale(joined.astype(jnp.float32), gains[1:2, :]).astype(
+                jnp.bfloat16
+            )
+            gather.start(part, z, x, own, partner)
+
+        sent = scatter_line(z, terms, from_pair, from_below, from_above, outgoing, pair_send,
+                            pair_recv, line_send, below_recv, above_recv, ready)
+        for arrivals in zip(*(gather.passing(p, z, x, own, partner) for p in range(PARTS))):
+            for part, (shard, onward) in enumerate(arrivals):
+                gather.copy(part, shard, partner, 2).wait_recv()
+                for out in onward:
+                    out.start()
+        for part in range(PARTS):
+            gather.arrive(part, z, x, own, partner)
+        for part in range(PARTS):
+            gather.drain(part, z, x, own, partner)
+        for out in sent:
+            out.wait_send()
+
+    at_place(body)
 
 
 def closing_kernel(terms, middle, handed,
                    from_pair, from_below, from_above, outgoing, pair_send, pair_recv,
-                   line_send, below_recv, above_recv, total, result, hand_send, hand_recv):
+                   line_send, below_recv, above_recv, result, hand_send, hand_recv):
     section, me = lax.axis_index("section"), lax.axis_index("expert")
     greet(True)
-    for z in range(LINE):
-
-        @pl.when(me // 2 == z)
-        def _(z=z):
-            scatter_line(z, terms, from_pair, from_below, from_above, outgoing, pair_send,
-                         pair_recv, line_send, below_recv, above_recv, total)
-
-    result[...] = (middle[...].astype(jnp.float32) + total[...]).astype(jnp.bfloat16)
-    hand = pltpu.make_async_remote_copy(
-        src_ref=result,
-        dst_ref=handed,
-        send_sem=hand_send,
-        recv_sem=hand_recv,
-        device_id=(lax.rem(section + 1, lax.axis_size("section")), me),
-        device_id_type=MESH,
-    )
-    hand.start()
-    hand.wait()
+
+    def hand(part):
+        return remote(
+            result.at[part], handed.at[part], hand_send.at[part], hand_recv.at[part],
+            me, lax.rem(section + 1, lax.axis_size("section")),
+        )
+
+    def ready(part, total):
+        result[part] = (middle[part].astype(jnp.float32) + total).astype(jnp.bfloat16)
+        hand(part).start()
+
+    def body(z, x, own, partner):
+        sent = scatter_line(z, terms, from_pair, from_below, from_above, outgoing, pair_send,
+                            pair_recv, line_send, below_recv, above_recv, ready)
+        for out in sent:
+            out.wait_send()
+
+    at_place(body)
+    for part in range(PARTS):
+        hand(part).wait()
 
 
 def in_vmem(count):
@@ -535,6 +504,7 @@
     head_dev = w_query.shape[2] // HD
     local_experts = w_gate_up.shape[1]
     gains = norm_gains[0]
+    own_acts = acts[0].reshape(PARTS, tok_rows // PARTS, width)
     tokens = tok_rows * GROUP
     keyval = w_keyval[0].transpose(1, 0, 2)
     keyval_rows = keyval.shape[1]
@@ -545,18 +515,18 @@
     row_piece, head_keyval, all_gates = pl.pallas_call(
         opening_kernel,
         out_shape=[
-            jax.ShapeDtypeStruct((1, GROUP, tok_rows, width), jnp.bfloat16),
+            jax.ShapeDtypeStruct((GROUP, PARTS, tok_rows // PARTS, width), jnp.bfloat16),
             jax.ShapeDtypeStruct((GROUP, keyval_rows, 2 * HD), jnp.bfloat16),
             jax.ShapeDtypeStruct(dense_gates.shape, jnp.float32),
         ],
         in_specs=in_vmem(4),
         out_specs=in_vmem(3),
         scratch_shapes=[
-            dma((1, GROUP, 3)), dma((1, GROUP)), dma((LINE,)), dma((GROUP,)), dma((LINE,)),
+            dma((PARTS, GROUP, 3)), dma((PARTS, GROUP)), dma((LINE,)), dma((GROUP,)), dma((LINE,)),
             dma((GROUP,)), dma((GROUP,)), dma((2,)),
         ],
         compiler_params=remote_params(0, 8),
-    )(acts[0], gains, keyval, dense_gates)
+    )(own_acts, gains, keyval, dense_gates)
     row_piece = row_piece.reshape(tokens, width)
     head_keyval = head_keyval.reshape(width, 2 * HD)
 
@@ -576,14 +546,14 @@
     mixer_rows, middle = pl.pallas_call(
         turning_kernel,
         out_shape=[
-            jax.ShapeDtypeStruct((GROUP, tok_rows, width), jnp.bfloat16),
-            jax.ShapeDtypeStruct((tok_rows, width), jnp.bfloat16),
+            jax.ShapeDtypeStruct((GROUP, PARTS, tok_rows // PARTS, width), jnp.bfloat16),
+            jax.ShapeDtypeStruct(own_acts.shape, jnp.bfloat16),
         ],
         in_specs=in_vmem(3),
         out_specs=in_vmem(2),
-        scratch_shapes=scatter_scratch(tok_rows, width) + [dma((GROUP, 3)), dma((GROUP,))],
+        scratch_shapes=scatter_scratch(tok_rows, width) + [dma((PARTS, GROUP, 3)), dma((PARTS, GROUP))],
         compiler_params=remote_params(1, 12),
-    )(terms.reshape(GROUP, tok_rows, width), acts[0], gains)
+    )(terms.reshape(GROUP, PARTS, tok_rows // PARTS, width), own_acts, gains)
     mixer_rows = mixer_rows.reshape(tokens, width)
 
     gates = all_gates.transpose(1, 0, 2).reshape(local_experts, tokens)
@@ -614,14 +584,14 @@
 
     handed = pl.pallas_call(
         closing_kernel,
-        out_shape=jax.ShapeDtypeStruct((tok_rows, width), jnp.bfloat16),
+        out_shape=jax.ShapeDtypeStruct(own_acts.shape, jnp.bfloat16),
         in_specs=in_vmem(2),
         out_specs=pl.BlockSpec(memory_space=pltpu.VMEM),
         scratch_shapes=scatter_scratch(tok_rows, width)
-        + [pltpu.VMEM((tok_rows, width), jnp.bfloat16), dma, dma],
+        + [pltpu.VMEM(own_acts.shape, jnp.bfloat16), dma((PARTS,)), dma((PARTS,))],
         compiler_params=remote_params(2, 10),
-    )(mixed.reshape(GROUP, tok_rows, width), middle)
-    return handed[None]
+    )(mixed.reshape(GROUP, PARTS, tok_rows // PARTS, width), middle)
+    return handed.reshape(1, tok_rows, width)
 
 
 def solution(mesh):

time: 170 us -> 159 us (0.935); the launches traced: 170 us -> 157 us
  Pallas kernels: 131 us -> 118 us
    pallas_call x3, Pallas kernels: 131 us -> 118 us  [the longest x1 45.8 us: per_device(): pl.pallas_call(turning_kernel, out_shape=[jax.ShapeDtypeStruct((GROUP, PA...]
where the time goes in v4:
time: 159 us; the launch traced here: 157 us
  Pallas kernels  118 us (74%)
  matrix products  30.5 us (19%)
  local copies, waits for them, and re-layouts  5.94 us (4%)
  other arithmetic  1.84 us (1%)
    pallas_call x1, Pallas kernels, per_device(): pl.pallas_call(turning_kernel, out_shape=[jax.ShapeDtypeStruct((GROUP, PA...  45.8 us
    pallas_call x1, Pallas kernels, per_device(): pl.pallas_call(opening_kernel, out_shape=[jax.ShapeDtypeStruct((GROUP, PA...  39 us
    pallas_call x1, Pallas kernels, per_device(): pl.pallas_call(closing_kernel, out_shape=jax.ShapeDtypeStruct(own_acts.sh...  33.3 us
    dot_general x1, matrix products, per_device(): jnp.einsum('esd,edf->esf', grouped, w_gate_up[0], preferred_element_type=...  15.2 us
    dot_general x1, matrix products, per_device(): jnp.dot(chosen.reshape(local_experts * slots, tokens).T, outputs.reshape(...  10.8 us
    unnamed x22, local copies, waits for them, and re-layouts  5.84 us

profile of v4, /device:TPU:9, one launch (start us, length us, event | category | flops | bytes accessed | tf_op | source)
XLA Modules:
  0.0 156.5 jit_solution(15695487319127979978)
XLA Ops:
  0.0 0.0 copy-start
  0.0 0.8 select_reduce_fusion.1
  0.8 1.1 copy.21
  1.9 0.0 copy-start.1
  1.9 0.9 copy-done.1
  2.9 0.0 copy-start.3
  2.9 0.7 copy-done.3
  3.6 0.0 copy-start.7
  3.6 39.0 %shard_map.103 = (bf16[8,2,32,2048]{3,2,1,0:T(8,128)(2,1)S(1)}, bf16[8,256,256]{2,1,0:T(8,128)(2,1)S(1)}, f32[8,4,64]{2,1,0:T(4,128)S(1)}) custom-call(bf16[2,32,2048]{2,1,0:T(8,128)(2,1)S(1)} %bitcast.79, f32[2,2048]{1,0:T(2,128)S(1)} %bitcast.82, bf16[4,256,256]{2,1,0:T(8,128)(2,1)S(1)} %bitcast.78, f32[8,4,64]{2,1,0:T(4,128)S(1)} %bitcast.84), custom_call_target="tpu_custom_call" | custom-call | tf_op jit(solution)/shard_map/pallas_call | solution.py:515
  42.7 0.8 fusion.62
  43.4 0.0 copy-done.7
  43.4 0.0 copy-start.8
  43.4 0.0 copy-start.9
  43.4 0.8 convolution_bitcast_fusion
  44.3 0.1 reshape.246
  44.4 0.2 fusion.17
  44.5 0.3 select_reduce_fusion
  44.8 0.6 fusion.52
  45.4 0.0 copy-done.9
  45.4 0.4 fusion.61
  45.8 0.0 copy-done.8
  45.8 0.0 copy-start.6
  45.8 1.0 copy-done.6
  46.8 0.2 fusion.19
  47.0 0.0 copy-done
  47.0 0.0 copy-start.2
  47.0 0.0 copy-start.4
  47.0 2.3 %convolution_convert_fusion.1 = bf16[512,2048]{1,0:T(8,128)(2,1)S(1)} fusion(bf16[1,128,2048]{2,1,0:T(8,128)(2,1)S(1)} %copy-done, f32[1,512,512]{1,2,0:T(8,128)} %copy-done.6, f32[512]{0:T(512)S(1)} %fusion.19, f32[512]{0:T(512)S(1)} %get-tuple-element.21, f32[512,256]{0,1:T(8,128)} %copy-done.8), kind=kOutput, calls=%fused_computation.8 | convolution fusion | flops 337444864 | bytes 3805184 | tf_op jit(solution)/shard_map/dot_general | solution.py:545
  49.4 0.0 copy-done.2
  49.4 0.0 copy-done.4
  49.4 45.8 %shard_map.104 = (bf16[8,2,32,2048]{3,2,1,0:T(8,128)(2,1)S(1)}, bf16[2,32,2048]{2,1,0:T(8,128)(2,1)S(1)}) custom-call(bf16[8,2,32,2048]{3,2,1,0:T(8,128)(2,1)S(1)} %bitcast.75, bf16[2,32,2048]{2,1,0:T(8,128)(2,1)S(1)} %bitcast.80, f32[2,2048]{1,0:T(2,128)S(1)} %bitcast.83), custom_call_target="tpu_custom_call" | custom-call | tf_op jit(solution)/shard_map/pallas_call | solution.py:546
  95.2 0.0 copy-start.5
  95.2 1.4 copy-done.5
  96.5 15.2 %fusion = f32[4,192,1536]{2,1,0:T(8,128)} fusion(bf16[1,4,2048,1536]{3,2,1,0:T(8,128)(2,1)} %param.15, bf16[512,2048,1]{1,0,2:T(8,128)(2,1)} %bitcast.86, s32[4,512]{1,0:T(4,128)S(1)} %fusion.17), kind=kOutput, calls=%fused_computation | convolution fusion | flops 6444417024 | bytes 31989760 | tf_op jit(solution)/shard_map/esd,edf->esf/dot_general | solution.py:572
  111.7 10.8 %bitcast_convert_fusion = bf16[512,2048]{1,0:T(8,128)(2,1)S(1)} fusion(bf16[1,4,768,2048]{3,2,1,0:T(8,128)(2,1)} %param.16, f32[4,192]{1,0:T(4,128)S(1)} %select_reduce_fusion, f32[4,192,1536]{2,1,0:T(8,128)} %fusion, s32[4,512]{1,0:T(4,128)S(1)} %fusion.17), kind=kOutput, calls=%fused_computation.5 | convolution fusion | flops 4034658304 | bytes 19409920 | tf_op jit(solution)/shard_map/dot_general | solution.py:579
  122.6 33.3 %shard_map.105 = bf16[2,32,2048]{2,1,0:T(8,128)(2,1)S(1)} custom-call(bf16[8,2,32,2048]{3,2,1,0:T(8,128)(2,1)S(1)} %bitcast.74, bf16[2,32,2048]{2,1,0:T(8,128)(2,1)S(1)} %get-tuple-element.14.middle), custom_call_target="tpu_custom_call" | custom-call | tf_op jit(solution)/shard_map/pallas_call | solution.py:585
  155.8 0.7 copy.23
  (4 shorter events, 0.0 us)
Async XLA Ops:
  0.0 47.0 %copy-start = (bf16[1,128,2048]{2,1,0:T(8,128)(2,1)S(1)}, bf16[1,128,2048]{2,1,0:T(8,128)(2,1)}, u32[]{:S(2)}) copy-start(bf16[1,128,2048]{2,1,0:T(8,128)(2,1)} %param.14) | copy-start | bytes 1572868
  1.9 1.0 copy-start.1
  2.9 0.7 copy-start.3
  3.6 39.8 %copy-start.7 = (bf16[1,2048,128]{2,1,0:T(8,128)(2,1)S(1)}, bf16[1,2048,128]{2,1,0:T(8,128)(2,1)}, u32[]{:S(2)}) copy-start(bf16[1,2048,128]{2,1,0:T(8,128)(2,1)} %param.12) | copy-start | bytes 1572868
  43.4 2.4 %copy-start.8 = (f32[512,256]{0,1:T(8,128)}, f32[512,256]{0,1:T(8,128)S(1)}, u32[]{:S(2)}) copy-start(f32[512,256]{0,1:T(8,128)S(1)} %fusion.62) | copy-start | bytes 1572868
  43.4 2.0 %copy-start.9 = (s32[1,512]{1,0:T(1,128)S(1)}, s32[1,512]{1,0:T(1,128)}, u32[]{:S(2)}) copy-start(s32[1,512]{1,0:T(1,128)} %param.19) | copy-start | bytes 6148
  45.8 1.0 copy-start.6
  47.0 2.4 %copy-start.2 = (bf16[1,64,2048]{2,1,0:T(8,128)(2,1)S(1)}, bf16[1,64,2048]{2,1,0:T(8,128)(2,1)}, u32[]{:S(2)}) copy-start(bf16[1,64,2048]{2,1,0:T(8,128)(2,1)} %param.10) | copy-start | bytes 786436
  47.0 2.4 %copy-start.4 = (f32[1,2,2048]{2,1,0:T(2,128)S(1)}, f32[1,2,2048]{2,1,0:T(2,128)}, u32[]{:S(2)}) copy-start(f32[1,2,2048]{2,1,0:T(2,128)} %param.11) | copy-start | bytes 49156
  95.2 1.4 copy-start.5
